TPU v7x, 768 devices: a whole 4x8x12 slice. The times are simulated.
768 devices in a mesh: dp: 64 (over z_hi, y, core), mp: 12 (over z_lo, x).
Axes of the slice: x: 4, y: 8, z: 12 (z_hi: 4, z_lo: 3; z = z_hi * 3 + z_lo), core: 2. Of those that a mesh axis runs over, the one named last changes fastest.
Arguments:
- token_factors: bfloat16 [12, 131072, 128], P('mp', 'dp'), may hold values from -6 to 6
- example_ids: int32 [64, 2048], P('dp'), may hold values from 0 to 7, never falling along the last dimension, each value on 1 to 1024 neighbouring positions
- left_factor: bfloat16 [12, 64, 64], P('mp'), may hold values from -0.75 to 0.75
- right_factor: bfloat16 [12, 64, 64], P('mp'), may hold values from -0.75 to 0.75
- query_features: bfloat16 [6144, 49152], P('dp', 'mp'), may hold values from -0.21875 to 0.21875
Outputs:
- influence: float32 [6144, 512], P(('dp', 'mp'))
Inputs may be any that keep to these rules, and one draw needn't show every extreme that they name: `example_ids`: each row is non-decreasing, and every example 0 to 7 has 1 to 1024 tokens in each block.
All inputs are finite; a program needn't handle non-finite values.
Results may differ from a plain program's by a relative error of at most 0.0029.
Values may be sent and summed in bfloat16 or wider, within the bound.
No kernel may reach another device: no remote copies, remote signals or barrier semaphores. Data moves between devices by JAX's collectives and lax.ppermute only.
A program may use at most 32 MiB of HBM per device.

v0:
```python
import jax
import jax.numpy as jnp
from jax import lax
from jax.sharding import PartitionSpec as P

EX_DEV = 8


def from_behind(array, axis, by):
    length = lax.axis_size(axis)
    return lax.ppermute(array, axis, [(i, (i + by) % length) for i in range(length)])


def score_block(queries, train_block):
    return lax.dot_general(
        queries, train_block, (((1,), (1,)), ((), ())), preferred_element_type=jnp.float32
    )


def shards(token_factors, example_ids, left_factor, right_factor, query_features):
    proj_rank = left_factor.shape[1]
    tokens_here = token_factors.shape[1]
    examples = EX_DEV
    labels = example_ids[0]
    onehot = labels[:, None] == jnp.arange(examples, dtype=jnp.int32)[None, :]
    selector = onehot.astype(jnp.bfloat16)
    counts = jnp.sum(onehot.astype(jnp.float32), axis=0)
    inputs = token_factors[0, :, :proj_rank]
    outputs = token_factors[0, :, proj_rank:]
    masked = (selector[:, :, None] * inputs[:, None, :]).reshape(tokens_here, examples * proj_rank)
    summed = lax.dot_general(
        outputs, masked, (((0,), (0,)), ((), ())), preferred_element_type=jnp.float32
    )
    gradient = (
        summed.reshape(proj_rank, examples, proj_rank).transpose(1, 0, 2) / counts[:, None, None]
    )
    precond = jnp.einsum(
        "ac,ecd,db->eab",
        left_factor[0].astype(jnp.float32),
        gradient,
        right_factor[0].astype(jnp.float32),
        precision=lax.Precision.HIGHEST,
    )
    pieces = precond.reshape(examples, proj_rank * proj_rank)
    features = pieces.astype(jnp.bfloat16)
    cycle_size = lax.axis_size("dp")
    position = lax.axis_index("dp")
    sources = jnp.arange(cycle_size, dtype=jnp.int32)
    local_scores = score_block(query_features, features)

    def advance_one(carry, unused):
        moved = from_behind(carry, "dp", 1)
        return (moved, score_block(query_features, moved))

    unused_carry, later = lax.scan(advance_one, features, None, length=cycle_size - 1)
    stacked = jnp.concatenate([local_scores[None], later], axis=0)
    columns = jnp.take(stacked, (position - sources) % cycle_size, axis=0)
    partial_value = columns.transpose(1, 0, 2).reshape(
        query_features.shape[0], cycle_size * examples
    )
    return lax.psum_scatter(partial_value, "mp", scatter_dimension=0, tiled=True)


def solution(mesh):
    placed = (
        P("mp", "dp", None),
        P("dp", None),
        P("mp", None, None),
        P("mp", None, None),
        P("dp", "mp"),
    )
    return jax.shard_map(
        shards, mesh=mesh, in_specs=placed, out_specs=P(("dp", "mp"), None), check_vma=False
    )
```

profile of v0, /device:TPU:1, one launch (start us, length us, event | category | flops | bytes accessed | tf_op | source)
XLA Modules:
  0.0 781.4 jit_solution(11969026048337235274)
XLA Ops:
  12.1 699.5 %while.12 = (s32[]{:T(128)}, bf16[8,4096]{1,0:T(8,128)(2,1)S(1)}, f32[63,96,8]{1,2,0:T(8,128)S(1)}, bf16[96,4096]{1,0:T(8,128)(2,1)S(1)}, s32[]{:T(128)}) while((s32[]{:T(128)}, bf16[8,4096]{1,0:T(8,128)(2,1)S(1)}, f32[63,96,8]{1,2,0:T(8,128)S(1)}, bf16[96,4096]{1,0:T(8,128)(2,1)S(1)}, s32[]{:T(128)}) %tuple.23), condition=%wide.region_2.3_spmd, body=%wide.region_1.2_spmd.sunk | while | flops 6291458 | bytes 1249393 | solution.py:55
  38.6 8.8 %collective-permute-done = bf16[8,4096]{1,0:T(8,128)(2,1)S(1)} collective-permute-done((bf16[8,4096]{1,0:T(8,128)(2,1)S(1)}, bf16[8,4096]{1,0:T(8,128)(2,1)S(1)}, u32[]{:S(2)}, u32[]{:S(2)}) %collective-permute-start) | collective-permute-done | bytes 65568 | tf_op jit(solution)/shard_map/while/body/eval_jaxpr/ppermute | solution.py:11
  49.6 9.1 %collective-permute-done = bf16[8,4096]{1,0:T(8,128)(2,1)S(1)} collective-permute-done((bf16[8,4096]{1,0:T(8,128)(2,1)S(1)}, bf16[8,4096]{1,0:T(8,128)(2,1)S(1)}, u32[]{:S(2)}, u32[]{:S(2)}) %collective-permute-start) | collective-permute-done | bytes 65568 | tf_op jit(solution)/shard_map/while/body/eval_jaxpr/ppermute | solution.py:11
  60.9 8.8 %collective-permute-done = bf16[8,4096]{1,0:T(8,128)(2,1)S(1)} collective-permute-done((bf16[8,4096]{1,0:T(8,128)(2,1)S(1)}, bf16[8,4096]{1,0:T(8,128)(2,1)S(1)}, u32[]{:S(2)}, u32[]{:S(2)}) %collective-permute-start) | collective-permute-done | bytes 65568 | tf_op jit(solution)/shard_map/while/body/eval_jaxpr/ppermute | solution.py:11
  72.0 8.8 %collective-permute-done = bf16[8,4096]{1,0:T(8,128)(2,1)S(1)} collective-permute-done((bf16[8,4096]{1,0:T(8,128)(2,1)S(1)}, bf16[8,4096]{1,0:T(8,128)(2,1)S(1)}, u32[]{:S(2)}, u32[]{:S(2)}) %collective-permute-start) | collective-permute-done | bytes 65568 | tf_op jit(solution)/shard_map/while/body/eval_jaxpr/ppermute | solution.py:11
  83.0 8.8 %collective-permute-done = bf16[8,4096]{1,0:T(8,128)(2,1)S(1)} collective-permute-done((bf16[8,4096]{1,0:T(8,128)(2,1)S(1)}, bf16[8,4096]{1,0:T(8,128)(2,1)S(1)}, u32[]{:S(2)}, u32[]{:S(2)}) %collective-permute-start) | collective-permute-done | bytes 65568 | tf_op jit(solution)/shard_map/while/body/eval_jaxpr/ppermute | solution.py:11
  105.0 8.8 %collective-permute-done = bf16[8,4096]{1,0:T(8,128)(2,1)S(1)} collective-permute-done((bf16[8,4096]{1,0:T(8,128)(2,1)S(1)}, bf16[8,4096]{1,0:T(8,128)(2,1)S(1)}, u32[]{:S(2)}, u32[]{:S(2)}) %collective-permute-start) | collective-permute-done | bytes 65568 | tf_op jit(solution)/shard_map/while/body/eval_jaxpr/ppermute | solution.py:11
  127.1 8.8 %collective-permute-done = bf16[8,4096]{1,0:T(8,128)(2,1)S(1)} collective-permute-done((bf16[8,4096]{1,0:T(8,128)(2,1)S(1)}, bf16[8,4096]{1,0:T(8,128)(2,1)S(1)}, u32[]{:S(2)}, u32[]{:S(2)}) %collective-permute-start) | collective-permute-done | bytes 65568 | tf_op jit(solution)/shard_map/while/body/eval_jaxpr/ppermute | solution.py:11
  149.1 9.5 %collective-permute-done = bf16[8,4096]{1,0:T(8,128)(2,1)S(1)} collective-permute-done((bf16[8,4096]{1,0:T(8,128)(2,1)S(1)}, bf16[8,4096]{1,0:T(8,128)(2,1)S(1)}, u32[]{:S(2)}, u32[]{:S(2)}) %collective-permute-start) | collective-permute-done | bytes 65568 | tf_op jit(solution)/shard_map/while/body/eval_jaxpr/ppermute | solution.py:11
  171.8 8.8 %collective-permute-done = bf16[8,4096]{1,0:T(8,128)(2,1)S(1)} collective-permute-done((bf16[8,4096]{1,0:T(8,128)(2,1)S(1)}, bf16[8,4096]{1,0:T(8,128)(2,1)S(1)}, u32[]{:S(2)}, u32[]{:S(2)}) %collective-permute-start) | collective-permute-done | bytes 65568 | tf_op jit(solution)/shard_map/while/body/eval_jaxpr/ppermute | solution.py:11
  204.9 8.8 %collective-permute-done = bf16[8,4096]{1,0:T(8,128)(2,1)S(1)} collective-permute-done((bf16[8,4096]{1,0:T(8,128)(2,1)S(1)}, bf16[8,4096]{1,0:T(8,128)(2,1)S(1)}, u32[]{:S(2)}, u32[]{:S(2)}) %collective-permute-start) | collective-permute-done | bytes 65568 | tf_op jit(solution)/shard_map/while/body/eval_jaxpr/ppermute | solution.py:11
  226.9 8.8 %collective-permute-done = bf16[8,4096]{1,0:T(8,128)(2,1)S(1)} collective-permute-done((bf16[8,4096]{1,0:T(8,128)(2,1)S(1)}, bf16[8,4096]{1,0:T(8,128)(2,1)S(1)}, u32[]{:S(2)}, u32[]{:S(2)}) %collective-permute-start) | collective-permute-done | bytes 65568 | tf_op jit(solution)/shard_map/while/body/eval_jaxpr/ppermute | solution.py:11
  237.9 8.8 %collective-permute-done = bf16[8,4096]{1,0:T(8,128)(2,1)S(1)} collective-permute-done((bf16[8,4096]{1,0:T(8,128)(2,1)S(1)}, bf16[8,4096]{1,0:T(8,128)(2,1)S(1)}, u32[]{:S(2)}, u32[]{:S(2)}) %collective-permute-start) | collective-permute-done | bytes 65568 | tf_op jit(solution)/shard_map/while/body/eval_jaxpr/ppermute | solution.py:11
  249.0 9.0 %collective-permute-done = bf16[8,4096]{1,0:T(8,128)(2,1)S(1)} collective-permute-done((bf16[8,4096]{1,0:T(8,128)(2,1)S(1)}, bf16[8,4096]{1,0:T(8,128)(2,1)S(1)}, u32[]{:S(2)}, u32[]{:S(2)}) %collective-permute-start) | collective-permute-done | bytes 65568 | tf_op jit(solution)/shard_map/while/body/eval_jaxpr/ppermute | solution.py:11
  271.2 8.8 %collective-permute-done = bf16[8,4096]{1,0:T(8,128)(2,1)S(1)} collective-permute-done((bf16[8,4096]{1,0:T(8,128)(2,1)S(1)}, bf16[8,4096]{1,0:T(8,128)(2,1)S(1)}, u32[]{:S(2)}, u32[]{:S(2)}) %collective-permute-start) | collective-permute-done | bytes 65568 | tf_op jit(solution)/shard_map/while/body/eval_jaxpr/ppermute | solution.py:11
  293.3 8.8 %collective-permute-done = bf16[8,4096]{1,0:T(8,128)(2,1)S(1)} collective-permute-done((bf16[8,4096]{1,0:T(8,128)(2,1)S(1)}, bf16[8,4096]{1,0:T(8,128)(2,1)S(1)}, u32[]{:S(2)}, u32[]{:S(2)}) %collective-permute-start) | collective-permute-done | bytes 65568 | tf_op jit(solution)/shard_map/while/body/eval_jaxpr/ppermute | solution.py:11
  315.3 8.8 %collective-permute-done = bf16[8,4096]{1,0:T(8,128)(2,1)S(1)} collective-permute-done((bf16[8,4096]{1,0:T(8,128)(2,1)S(1)}, bf16[8,4096]{1,0:T(8,128)(2,1)S(1)}, u32[]{:S(2)}, u32[]{:S(2)}) %collective-permute-start) | collective-permute-done | bytes 65568 | tf_op jit(solution)/shard_map/while/body/eval_jaxpr/ppermute | solution.py:11
  326.3 8.8 %collective-permute-done = bf16[8,4096]{1,0:T(8,128)(2,1)S(1)} collective-permute-done((bf16[8,4096]{1,0:T(8,128)(2,1)S(1)}, bf16[8,4096]{1,0:T(8,128)(2,1)S(1)}, u32[]{:S(2)}, u32[]{:S(2)}) %collective-permute-start) | collective-permute-done | bytes 65568 | tf_op jit(solution)/shard_map/while/body/eval_jaxpr/ppermute | solution.py:11
  348.4 9.5 %collective-permute-done = bf16[8,4096]{1,0:T(8,128)(2,1)S(1)} collective-permute-done((bf16[8,4096]{1,0:T(8,128)(2,1)S(1)}, bf16[8,4096]{1,0:T(8,128)(2,1)S(1)}, u32[]{:S(2)}, u32[]{:S(2)}) %collective-permute-start) | collective-permute-done | bytes 65568 | tf_op jit(solution)/shard_map/while/body/eval_jaxpr/ppermute | solution.py:11
  371.1 8.8 %collective-permute-done = bf16[8,4096]{1,0:T(8,128)(2,1)S(1)} collective-permute-done((bf16[8,4096]{1,0:T(8,128)(2,1)S(1)}, bf16[8,4096]{1,0:T(8,128)(2,1)S(1)}, u32[]{:S(2)}, u32[]{:S(2)}) %collective-permute-start) | collective-permute-done | bytes 65568 | tf_op jit(solution)/shard_map/while/body/eval_jaxpr/ppermute | solution.py:11
  448.2 9.5 %collective-permute-done = bf16[8,4096]{1,0:T(8,128)(2,1)S(1)} collective-permute-done((bf16[8,4096]{1,0:T(8,128)(2,1)S(1)}, bf16[8,4096]{1,0:T(8,128)(2,1)S(1)}, u32[]{:S(2)}, u32[]{:S(2)}) %collective-permute-start) | collective-permute-done | bytes 65568 | tf_op jit(solution)/shard_map/while/body/eval_jaxpr/ppermute | solution.py:11
  548.1 8.8 %collective-permute-done = bf16[8,4096]{1,0:T(8,128)(2,1)S(1)} collective-permute-done((bf16[8,4096]{1,0:T(8,128)(2,1)S(1)}, bf16[8,4096]{1,0:T(8,128)(2,1)S(1)}, u32[]{:S(2)}, u32[]{:S(2)}) %collective-permute-start) | collective-permute-done | bytes 65568 | tf_op jit(solution)/shard_map/while/body/eval_jaxpr/ppermute | solution.py:11
  559.1 9.0 %collective-permute-done = bf16[8,4096]{1,0:T(8,128)(2,1)S(1)} collective-permute-done((bf16[8,4096]{1,0:T(8,128)(2,1)S(1)}, bf16[8,4096]{1,0:T(8,128)(2,1)S(1)}, u32[]{:S(2)}, u32[]{:S(2)}) %collective-permute-start) | collective-permute-done | bytes 65568 | tf_op jit(solution)/shard_map/while/body/eval_jaxpr/ppermute | solution.py:11
  713.2 61.4 %reduce-scatter.4.cloned.1.call-done = f32[8,512]{1,0:T(8,128)} async-done(((f32[96,512]{1,0:T(8,128)}), f32[8,512]{1,0:T(8,128)}) %reduce-scatter.4.cloned.1.call-update) | async-done | bytes 16400 | tf_op jit(solution)/shard_map/reduce_scatter | solution.py:61
  (259 shorter events, 510.0 us)
Async XLA Ops:
  6.5 768.1 %reduce-scatter.4.cloned.1.call-start = ((), (), s32[]{:S(2)}) async-start(), calls=%async_computation.1 | async-start | bytes 212992 | tf_op jit(solution)/shard_map/reduce_scatter | solution.py:61
  12.1 13.2 %collective-permute-start = (bf16[8,4096]{1,0:T(8,128)(2,1)S(1)}, bf16[8,4096]{1,0:T(8,128)(2,1)S(1)}, u32[]{:S(2)}, u32[]{:S(2)}) collective-permute-start(bf16[8,4096]{1,0:T(8,128)(2,1)S(1)} %get-tuple-element.67), channel_id=1, source_target_pairs={{0,12},{12,24},{24,36},{36,48},{48,60},{60,72},{72,84},{84,96},{96... | collective-permute-start | bytes 196616 | tf_op jit(solution)/shard_map/while/body/eval_jaxpr/ppermute | solution.py:11
  25.6 10.7 %collective-permute-start = (bf16[8,4096]{1,0:T(8,128)(2,1)S(1)}, bf16[8,4096]{1,0:T(8,128)(2,1)S(1)}, u32[]{:S(2)}, u32[]{:S(2)}) collective-permute-start(bf16[8,4096]{1,0:T(8,128)(2,1)S(1)} %get-tuple-element.67), channel_id=1, source_target_pairs={{0,12},{12,24},{24,36},{36,48},{48,60},{60,72},{72,84},{84,96},{96... | collective-permute-start | bytes 196616 | tf_op jit(solution)/shard_map/while/body/eval_jaxpr/ppermute | solution.py:11
  36.6 10.7 %collective-permute-start = (bf16[8,4096]{1,0:T(8,128)(2,1)S(1)}, bf16[8,4096]{1,0:T(8,128)(2,1)S(1)}, u32[]{:S(2)}, u32[]{:S(2)}) collective-permute-start(bf16[8,4096]{1,0:T(8,128)(2,1)S(1)} %get-tuple-element.67), channel_id=1, source_target_pairs={{0,12},{12,24},{24,36},{36,48},{48,60},{60,72},{72,84},{84,96},{96... | collective-permute-start | bytes 196616 | tf_op jit(solution)/shard_map/while/body/eval_jaxpr/ppermute | solution.py:11
  47.7 11.0 %collective-permute-start = (bf16[8,4096]{1,0:T(8,128)(2,1)S(1)}, bf16[8,4096]{1,0:T(8,128)(2,1)S(1)}, u32[]{:S(2)}, u32[]{:S(2)}) collective-permute-start(bf16[8,4096]{1,0:T(8,128)(2,1)S(1)} %get-tuple-element.67), channel_id=1, source_target_pairs={{0,12},{12,24},{24,36},{36,48},{48,60},{60,72},{72,84},{84,96},{96... | collective-permute-start | bytes 196616 | tf_op jit(solution)/shard_map/while/body/eval_jaxpr/ppermute | solution.py:11
  59.0 10.7 %collective-permute-start = (bf16[8,4096]{1,0:T(8,128)(2,1)S(1)}, bf16[8,4096]{1,0:T(8,128)(2,1)S(1)}, u32[]{:S(2)}, u32[]{:S(2)}) collective-permute-start(bf16[8,4096]{1,0:T(8,128)(2,1)S(1)} %get-tuple-element.67), channel_id=1, source_target_pairs={{0,12},{12,24},{24,36},{36,48},{48,60},{60,72},{72,84},{84,96},{96... | collective-permute-start | bytes 196616 | tf_op jit(solution)/shard_map/while/body/eval_jaxpr/ppermute | solution.py:11
  70.0 10.7 %collective-permute-start = (bf16[8,4096]{1,0:T(8,128)(2,1)S(1)}, bf16[8,4096]{1,0:T(8,128)(2,1)S(1)}, u32[]{:S(2)}, u32[]{:S(2)}) collective-permute-start(bf16[8,4096]{1,0:T(8,128)(2,1)S(1)} %get-tuple-element.67), channel_id=1, source_target_pairs={{0,12},{12,24},{24,36},{36,48},{48,60},{60,72},{72,84},{84,96},{96... | collective-permute-start | bytes 196616 | tf_op jit(solution)/shard_map/while/body/eval_jaxpr/ppermute | solution.py:11
  81.1 10.7 %collective-permute-start = (bf16[8,4096]{1,0:T(8,128)(2,1)S(1)}, bf16[8,4096]{1,0:T(8,128)(2,1)S(1)}, u32[]{:S(2)}, u32[]{:S(2)}) collective-permute-start(bf16[8,4096]{1,0:T(8,128)(2,1)S(1)} %get-tuple-element.67), channel_id=1, source_target_pairs={{0,12},{12,24},{24,36},{36,48},{48,60},{60,72},{72,84},{84,96},{96... | collective-permute-start | bytes 196616 | tf_op jit(solution)/shard_map/while/body/eval_jaxpr/ppermute | solution.py:11
  92.1 10.7 %collective-permute-start = (bf16[8,4096]{1,0:T(8,128)(2,1)S(1)}, bf16[8,4096]{1,0:T(8,128)(2,1)S(1)}, u32[]{:S(2)}, u32[]{:S(2)}) collective-permute-start(bf16[8,4096]{1,0:T(8,128)(2,1)S(1)} %get-tuple-element.67), channel_id=1, source_target_pairs={{0,12},{12,24},{24,36},{36,48},{48,60},{60,72},{72,84},{84,96},{96... | collective-permute-start | bytes 196616 | tf_op jit(solution)/shard_map/while/body/eval_jaxpr/ppermute | solution.py:11
  103.1 10.7 %collective-permute-start = (bf16[8,4096]{1,0:T(8,128)(2,1)S(1)}, bf16[8,4096]{1,0:T(8,128)(2,1)S(1)}, u32[]{:S(2)}, u32[]{:S(2)}) collective-permute-start(bf16[8,4096]{1,0:T(8,128)(2,1)S(1)} %get-tuple-element.67), channel_id=1, source_target_pairs={{0,12},{12,24},{24,36},{36,48},{48,60},{60,72},{72,84},{84,96},{96... | collective-permute-start | bytes 196616 | tf_op jit(solution)/shard_map/while/body/eval_jaxpr/ppermute | solution.py:11
  114.1 10.7 %collective-permute-start = (bf16[8,4096]{1,0:T(8,128)(2,1)S(1)}, bf16[8,4096]{1,0:T(8,128)(2,1)S(1)}, u32[]{:S(2)}, u32[]{:S(2)}) collective-permute-start(bf16[8,4096]{1,0:T(8,128)(2,1)S(1)} %get-tuple-element.67), channel_id=1, source_target_pairs={{0,12},{12,24},{24,36},{36,48},{48,60},{60,72},{72,84},{84,96},{96... | collective-permute-start | bytes 196616 | tf_op jit(solution)/shard_map/while/body/eval_jaxpr/ppermute | solution.py:11
  125.1 10.7 %collective-permute-start = (bf16[8,4096]{1,0:T(8,128)(2,1)S(1)}, bf16[8,4096]{1,0:T(8,128)(2,1)S(1)}, u32[]{:S(2)}, u32[]{:S(2)}) collective-permute-start(bf16[8,4096]{1,0:T(8,128)(2,1)S(1)} %get-tuple-element.67), channel_id=1, source_target_pairs={{0,12},{12,24},{24,36},{36,48},{48,60},{60,72},{72,84},{84,96},{96... | collective-permute-start | bytes 196616 | tf_op jit(solution)/shard_map/while/body/eval_jaxpr/ppermute | solution.py:11
  136.2 10.7 %collective-permute-start = (bf16[8,4096]{1,0:T(8,128)(2,1)S(1)}, bf16[8,4096]{1,0:T(8,128)(2,1)S(1)}, u32[]{:S(2)}, u32[]{:S(2)}) collective-permute-start(bf16[8,4096]{1,0:T(8,128)(2,1)S(1)} %get-tuple-element.67), channel_id=1, source_target_pairs={{0,12},{12,24},{24,36},{36,48},{48,60},{60,72},{72,84},{84,96},{96... | collective-permute-start | bytes 196616 | tf_op jit(solution)/shard_map/while/body/eval_jaxpr/ppermute | solution.py:11
  147.2 11.4 %collective-permute-start = (bf16[8,4096]{1,0:T(8,128)(2,1)S(1)}, bf16[8,4096]{1,0:T(8,128)(2,1)S(1)}, u32[]{:S(2)}, u32[]{:S(2)}) collective-permute-start(bf16[8,4096]{1,0:T(8,128)(2,1)S(1)} %get-tuple-element.67), channel_id=1, source_target_pairs={{0,12},{12,24},{24,36},{36,48},{48,60},{60,72},{72,84},{84,96},{96... | collective-permute-start | bytes 196616 | tf_op jit(solution)/shard_map/while/body/eval_jaxpr/ppermute | solution.py:11
  158.9 10.7 %collective-permute-start = (bf16[8,4096]{1,0:T(8,128)(2,1)S(1)}, bf16[8,4096]{1,0:T(8,128)(2,1)S(1)}, u32[]{:S(2)}, u32[]{:S(2)}) collective-permute-start(bf16[8,4096]{1,0:T(8,128)(2,1)S(1)} %get-tuple-element.67), channel_id=1, source_target_pairs={{0,12},{12,24},{24,36},{36,48},{48,60},{60,72},{72,84},{84,96},{96... | collective-permute-start | bytes 196616 | tf_op jit(solution)/shard_map/while/body/eval_jaxpr/ppermute | solution.py:11
  169.9 10.7 %collective-permute-start = (bf16[8,4096]{1,0:T(8,128)(2,1)S(1)}, bf16[8,4096]{1,0:T(8,128)(2,1)S(1)}, u32[]{:S(2)}, u32[]{:S(2)}) collective-permute-start(bf16[8,4096]{1,0:T(8,128)(2,1)S(1)} %get-tuple-element.67), channel_id=1, source_target_pairs={{0,12},{12,24},{24,36},{36,48},{48,60},{60,72},{72,84},{84,96},{96... | collective-permute-start | bytes 196616 | tf_op jit(solution)/shard_map/while/body/eval_jaxpr/ppermute | solution.py:11
  236.0 10.7 %collective-permute-start = (bf16[8,4096]{1,0:T(8,128)(2,1)S(1)}, bf16[8,4096]{1,0:T(8,128)(2,1)S(1)}, u32[]{:S(2)}, u32[]{:S(2)}) collective-permute-start(bf16[8,4096]{1,0:T(8,128)(2,1)S(1)} %get-tuple-element.67), channel_id=1, source_target_pairs={{0,12},{12,24},{24,36},{36,48},{48,60},{60,72},{72,84},{84,96},{96... | collective-permute-start | bytes 196616 | tf_op jit(solution)/shard_map/while/body/eval_jaxpr/ppermute | solution.py:11
  247.0 10.9 %collective-permute-start = (bf16[8,4096]{1,0:T(8,128)(2,1)S(1)}, bf16[8,4096]{1,0:T(8,128)(2,1)S(1)}, u32[]{:S(2)}, u32[]{:S(2)}) collective-permute-start(bf16[8,4096]{1,0:T(8,128)(2,1)S(1)} %get-tuple-element.67), channel_id=1, source_target_pairs={{0,12},{12,24},{24,36},{36,48},{48,60},{60,72},{72,84},{84,96},{96... | collective-permute-start | bytes 196616 | tf_op jit(solution)/shard_map/while/body/eval_jaxpr/ppermute | solution.py:11
  313.4 10.7 %collective-permute-start = (bf16[8,4096]{1,0:T(8,128)(2,1)S(1)}, bf16[8,4096]{1,0:T(8,128)(2,1)S(1)}, u32[]{:S(2)}, u32[]{:S(2)}) collective-permute-start(bf16[8,4096]{1,0:T(8,128)(2,1)S(1)} %get-tuple-element.67), channel_id=1, source_target_pairs={{0,12},{12,24},{24,36},{36,48},{48,60},{60,72},{72,84},{84,96},{96... | collective-permute-start | bytes 196616 | tf_op jit(solution)/shard_map/while/body/eval_jaxpr/ppermute | solution.py:11
  346.4 11.4 %collective-permute-start = (bf16[8,4096]{1,0:T(8,128)(2,1)S(1)}, bf16[8,4096]{1,0:T(8,128)(2,1)S(1)}, u32[]{:S(2)}, u32[]{:S(2)}) collective-permute-start(bf16[8,4096]{1,0:T(8,128)(2,1)S(1)} %get-tuple-element.67), channel_id=1, source_target_pairs={{0,12},{12,24},{24,36},{36,48},{48,60},{60,72},{72,84},{84,96},{96... | collective-permute-start | bytes 196616 | tf_op jit(solution)/shard_map/while/body/eval_jaxpr/ppermute | solution.py:11
  446.3 11.4 %collective-permute-start = (bf16[8,4096]{1,0:T(8,128)(2,1)S(1)}, bf16[8,4096]{1,0:T(8,128)(2,1)S(1)}, u32[]{:S(2)}, u32[]{:S(2)}) collective-permute-start(bf16[8,4096]{1,0:T(8,128)(2,1)S(1)} %get-tuple-element.67), channel_id=1, source_target_pairs={{0,12},{12,24},{24,36},{36,48},{48,60},{60,72},{72,84},{84,96},{96... | collective-permute-start | bytes 196616 | tf_op jit(solution)/shard_map/while/body/eval_jaxpr/ppermute | solution.py:11
  458.0 10.7 %collective-permute-start = (bf16[8,4096]{1,0:T(8,128)(2,1)S(1)}, bf16[8,4096]{1,0:T(8,128)(2,1)S(1)}, u32[]{:S(2)}, u32[]{:S(2)}) collective-permute-start(bf16[8,4096]{1,0:T(8,128)(2,1)S(1)} %get-tuple-element.67), channel_id=1, source_target_pairs={{0,12},{12,24},{24,36},{36,48},{48,60},{60,72},{72,84},{84,96},{96... | collective-permute-start | bytes 196616 | tf_op jit(solution)/shard_map/while/body/eval_jaxpr/ppermute | solution.py:11
  546.1 10.7 %collective-permute-start = (bf16[8,4096]{1,0:T(8,128)(2,1)S(1)}, bf16[8,4096]{1,0:T(8,128)(2,1)S(1)}, u32[]{:S(2)}, u32[]{:S(2)}) collective-permute-start(bf16[8,4096]{1,0:T(8,128)(2,1)S(1)} %get-tuple-element.67), channel_id=1, source_target_pairs={{0,12},{12,24},{24,36},{36,48},{48,60},{60,72},{72,84},{84,96},{96... | collective-permute-start | bytes 196616 | tf_op jit(solution)/shard_map/while/body/eval_jaxpr/ppermute | solution.py:11
  557.2 10.9 %collective-permute-start = (bf16[8,4096]{1,0:T(8,128)(2,1)S(1)}, bf16[8,4096]{1,0:T(8,128)(2,1)S(1)}, u32[]{:S(2)}, u32[]{:S(2)}) collective-permute-start(bf16[8,4096]{1,0:T(8,128)(2,1)S(1)} %get-tuple-element.67), channel_id=1, source_target_pairs={{0,12},{12,24},{24,36},{36,48},{48,60},{60,72},{72,84},{84,96},{96... | collective-permute-start | bytes 196616 | tf_op jit(solution)/shard_map/while/body/eval_jaxpr/ppermute | solution.py:11
  (44 other events, 438.0 us)
Sparse Core Ops, SparseCore 0:
  713.4 61.1 reduce-scatter.3
where the time goes:
time: 796 us; the launch traced here: 781 us
  waiting for transfers between devices  617 us (78%)
  starting transfers between devices  124 us (16%)
  matrix products  21.1 us (3%)
  between operations  13.5 us (2%)
    ppermute x63, waiting for transfers between devices, from_behind(): lax.ppermute(array, axis, [(i, (i + by) % length) for i in range(length)])  555 us
    ppermute x63, starting transfers between devices, from_behind(): lax.ppermute(array, axis, [(i, (i + by) % length) for i in range(length)])  124 us
    reduce_scatter x1, waiting for transfers between devices, shards(): lax.psum_scatter(partial_value, 'mp', scatter_dimension=0, tiled=True)  61.4 us
    dot_general x64, matrix products, score_block(): lax.dot_general(queries, train_block, (((1,), (1,)), ((), ())), preferred...  19.3 us
  transfers between devices with their start and end apart: 64, of which 64 were waited for; matrix products, arithmetic and copies ran while one was open for 0% of the time, Pallas kernels for 0%

commit v1 on v0

--- a/solution.py
+++ b/solution.py
@@ -4,11 +4,6 @@
 from jax.sharding import PartitionSpec as P
 
 EX_DEV = 8
-
-
-def from_behind(array, axis, by):
-    length = lax.axis_size(axis)
-    return lax.ppermute(array, axis, [(i, (i + by) % length) for i in range(length)])
 
 
 def score_block(queries, train_block):
@@ -43,22 +38,12 @@
     )
     pieces = precond.reshape(examples, proj_rank * proj_rank)
     features = pieces.astype(jnp.bfloat16)
-    cycle_size = lax.axis_size("dp")
-    position = lax.axis_index("dp")
-    sources = jnp.arange(cycle_size, dtype=jnp.int32)
-    local_scores = score_block(query_features, features)
-
-    def advance_one(carry, unused):
-        moved = from_behind(carry, "dp", 1)
-        return (moved, score_block(query_features, moved))
-
-    unused_carry, later = lax.scan(advance_one, features, None, length=cycle_size - 1)
-    stacked = jnp.concatenate([local_scores[None], later], axis=0)
-    columns = jnp.take(stacked, (position - sources) % cycle_size, axis=0)
-    partial_value = columns.transpose(1, 0, 2).reshape(
-        query_features.shape[0], cycle_size * examples
-    )
-    return lax.psum_scatter(partial_value, "mp", scatter_dimension=0, tiled=True)
+    gathered = lax.all_gather(features, "dp", axis=0, tiled=True)
+    partial_value = score_block(query_features, gathered)
+    members = lax.axis_size("mp")
+    parts = partial_value.reshape(members, partial_value.shape[0] // members, -1)
+    traded = lax.all_to_all(parts, "mp", 0, 0, tiled=False)
+    return jnp.sum(traded, axis=0)
 
 
 def solution(mesh):

time: 796 us -> 147 us (0.18); the launches traced: 781 us -> 146 us
  waiting for transfers between devices: 617 us -> 112 us
  starting transfers between devices: 124 us -> 0.01 us
  matrix products: 21.1 us -> 5.11 us
  blocking collectives: 0 us -> 10.5 us
    ppermute x63 -> x0, waiting for transfers between devices: 555 us -> none  [from_behind(): lax.ppermute(array, axis, [(i, (i + by) % length) for i in range(length)])]
    ppermute x63 -> x0, starting transfers between devices: 124 us -> none  [from_behind(): lax.ppermute(array, axis, [(i, (i + by) % length) for i in range(length)])]
    all_gather x0 -> x1, waiting for transfers between devices: none -> 112 us  [shards(): gathered = lax.all_gather(features, 'dp', axis=0, tiled=True)]
    reduce_scatter x1 -> x0, waiting for transfers between devices: 61.4 us -> none  [shards(): lax.psum_scatter(partial_value, 'mp', scatter_dimension=0, tiled=True)]
    dot_general x64 -> x1, matrix products: 19.3 us -> 3.61 us  [score_block(): lax.dot_general(queries, train_block, (((1,), (1,)), ((), ())), preferred...]
    all_to_all x0 -> x1, blocking collectives: none -> 10.5 us  [shards(): traded = lax.all_to_all(parts, 'mp', 0, 0, tiled=False)]
  transfers between devices with their start and end apart: 64 -> 1, of which waited for: 64 -> 1; matrix products, arithmetic and copies ran while one was open for 0% -> 0% of each run, Pallas kernels for 0% -> 0%
where the time goes in v1:
time: 147 us; the launch traced here: 146 us
  waiting for transfers between devices  112 us (76%)
  between operations  13.5 us (9%)
  blocking collectives  10.5 us (7%)
  matrix products  5.11 us (3%)
  other arithmetic  2.49 us (2%)
  local copies, waits for them, and re-layouts  2.27 us (2%)
    all_gather x1, waiting for transfers between devices, shards(): gathered = lax.all_gather(features, 'dp', axis=0, tiled=True)  112 us
    all_to_all x1, blocking collectives, shards(): traded = lax.all_to_all(parts, 'mp', 0, 0, tiled=False)  10.5 us
    dot_general x1, matrix products, score_block(): lax.dot_general(queries, train_block, (((1,), (1,)), ((), ())), preferred...  3.61 us
  transfers between devices with their start and end apart: 1, of which 1 were waited for; matrix products, arithmetic and copies ran while one was open for 0% of the time, Pallas kernels for 0%

profile of v1, /device:TPU:1, one launch (start us, length us, event | category | flops | bytes accessed | tf_op | source)
XLA Modules:
  0.0 145.8 jit_solution(17734344656665601229)
XLA Ops:
  6.5 0.0 copy-start
  6.5 0.0 all-gather.2.cloned.1.call-start
  6.5 0.9 convert_reduce_fusion
  7.4 0.7 fusion.4
  8.2 0.0 copy-start.1
  8.2 1.1 slice_bitcast_fusion
  9.3 0.2 copy.6
  9.5 0.2 broadcast_multiply_fusion
  9.7 0.0 copy-start.2
  9.7 0.0 copy-done.1
  9.7 0.0 copy-start.3
  9.7 0.9 convolution_bitcast_fusion.1
  10.7 0.1 reshape.48
  10.8 0.1 divide_bitcast_fusion
  10.9 0.0 copy-done.2
  10.9 0.3 fusion.2
  11.2 0.0 copy-done.3
  11.2 0.2 convolution_convert_fusion
  11.5 0.8 convert_element_type.21
  12.3 0.0 all-gather.2.cloned.1.call-update
  12.3 111.9 %all-gather.2.cloned.1.call-done = bf16[512,4096]{1,0:T(8,128)(2,1)} async-done(((bf16[8,4096]{1,0:T(8,128)(2,1)}), bf16[512,4096]{1,0:T(8,128)(2,1)}) %all-gather.2.cloned.1.call-update) | async-done | bytes 4194320 | tf_op jit(solution)/shard_map/all_gather | solution.py:41
  124.2 3.6 %convolution_bitcast_fusion = f32[12,8,512]{2,1,0:T(8,128)S(1)} fusion(bf16[512,4096]{1,0:T(8,128)(2,1)} %all-gather.2.cloned.1.call-done, bf16[96,4096]{1,0:T(8,128)(2,1)S(1)} %copy-done), kind=kOutput, calls=%fused_computation | convolution fusion | flops 402653184 | bytes 5177344 | tf_op jit(solution)/shard_map/dot_general | solution.py:10
  127.8 10.5 %all_to_all.5 = f32[12,8,512]{2,1,0:T(8,128)S(1)} all-to-all(f32[12,8,512]{2,1,0:T(8,128)S(1)} %convolution_bitcast_fusion), channel_id=1, replica_groups=mesh['dp'=64,'mp'=12] {'mp'}, dimensions={0} | all-to-all | bytes 393216 | tf_op jit(solution)/shard_map/all_to_all | solution.py:45
  138.4 0.6 reduce_sum.19
  (1 shorter events, 0.0 us)
Async XLA Ops:
  6.5 117.7 %copy-start = (bf16[96,4096]{1,0:T(8,128)(2,1)S(1)}, bf16[96,4096]{1,0:T(8,128)(2,1)}, u32[]{:S(2)}) copy-start(bf16[96,4096]{1,0:T(8,128)(2,1)} %param.9) | copy-start | bytes 2359300
  6.5 117.7 %all-gather.2.cloned.1.call-start = ((), (), s32[]{:S(2)}) async-start(), calls=%async_computation.1 | async-start | bytes 4259840 | tf_op jit(solution)/shard_map/all_gather | solution.py:41
  8.2 1.5 %copy-start.1 = (bf16[1,2048,128]{2,1,0:T(8,128)(2,1)S(1)}, bf16[1,2048,128]{2,1,0:T(8,128)(2,1)}, u32[]{:S(2)}) copy-start(bf16[1,2048,128]{2,1,0:T(8,128)(2,1)} %param.5) | copy-start | bytes 1572868
  9.7 1.2 copy-start.2
  9.7 1.5 %copy-start.3 = (bf16[1,64,64]{2,1,0:T(8,128)(2,1)S(1)}, bf16[1,64,64]{2,1,0:T(8,128)(2,1)}, u32[]{:S(2)}) copy-start(bf16[1,64,64]{2,1,0:T(8,128)(2,1)} %param.8) | copy-start | bytes 24580
Sparse Core Ops, SparseCore 0:
  12.4 111.7 all-gather.1

commit v2 on v1

v2 whole, which is shorter than its diff:
```python
import jax
import jax.numpy as jnp
from jax import lax
from jax.sharding import Mesh, PartitionSpec as P

EX_DEV = 8
Z_HI, Y, CORE, Z_LO, X = 4, 8, 2, 3, 4
DP = ("zh", "y", "core")
MP = ("zl", "x")


def from_behind(array, axis, by):
    length = lax.axis_size(axis)
    return lax.ppermute(array, axis, [(i, (i + by) % length) for i in range(length)])


def block_features(token_factors, example_ids, left_factor, right_factor):
    proj_rank = left_factor.shape[1]
    tokens_here = token_factors.shape[1]
    examples = EX_DEV
    labels = example_ids[0]
    onehot = labels[:, None] == jnp.arange(examples, dtype=jnp.int32)[None, :]
    selector = onehot.astype(jnp.bfloat16)
    counts = jnp.sum(onehot.astype(jnp.float32), axis=0)
    inputs = token_factors[0, :, :proj_rank]
    outputs = token_factors[0, :, proj_rank:]
    masked = (selector[:, :, None] * inputs[:, None, :]).reshape(tokens_here, examples * proj_rank)
    summed = lax.dot_general(
        outputs, masked, (((0,), (0,)), ((), ())), preferred_element_type=jnp.float32
    )
    gradient = (
        summed.reshape(proj_rank, examples, proj_rank).transpose(1, 0, 2) / counts[:, None, None]
    )
    precond = jnp.einsum(
        "ac,ecd,db->eab",
        left_factor[0].astype(jnp.float32),
        gradient,
        right_factor[0].astype(jnp.float32),
        precision=lax.Precision.HIGHEST,
    )
    return precond.reshape(examples, proj_rank * proj_rank).astype(jnp.bfloat16)


def both_cores(mine, partner, core):
    return jnp.where(
        core == 0,
        jnp.concatenate([mine, partner], axis=0),
        jnp.concatenate([partner, mine], axis=0),
    )


def placing(width, position):
    source = lax.broadcasted_iota(jnp.int32, (width, width), 0)
    result = lax.broadcasted_iota(jnp.int32, (width, width), 1)
    example = source % EX_DEV
    z_hi = source // EX_DEV % Z_HI
    arrival = source // (EX_DEV * Z_HI) % Y
    core = source // (EX_DEV * Z_HI * Y)
    offset = jnp.where(arrival % 2 == 0, arrival // 2, Y - (arrival + 1) // 2)
    y = (position + offset) % Y
    return (result == ((z_hi * Y + y) * CORE + core) * EX_DEV + example).astype(jnp.float32)


def shards(token_factors, example_ids, left_factor, right_factor, query_features):
    rows = query_features.shape[0]
    features = block_features(token_factors, example_ids, left_factor, right_factor)
    partner = from_behind(query_features, "core", 1)
    queries = both_cores(query_features, partner, lax.axis_index("core"))

    copies = jnp.broadcast_to(features[None], (Z_HI,) + features.shape)
    column = lax.all_to_all(copies, "zh", 0, 0, tiled=False).reshape(Z_HI * EX_DEV, -1)

    up = down = column
    pieces = [column]
    for step in range(1, Y // 2):
        up = from_behind(up, "y", 1)
        down = from_behind(down, "y", -1)
        pieces += [up, down]
    half = column.shape[0] // 2
    pieces += [from_behind(up[:half], "y", 1), from_behind(down[half:], "y", -1)]

    scores = [
        lax.dot_general(
            queries, piece, (((1,), (1,)), ((), ())), preferred_element_type=jnp.float32
        ).astype(jnp.bfloat16)
        for piece in pieces
    ]
    members = Z_LO * X
    parts = jnp.concatenate(scores, axis=1).reshape(CORE * members, rows // members, -1)
    traded = lax.all_to_all(parts, ("core",) + MP, 0, 0, tiled=False)
    totals = jnp.sum(
        traded.astype(jnp.float32).reshape(CORE, members, rows // members, -1), axis=1
    )
    flat = jnp.concatenate([totals[0], totals[1]], axis=1)
    place = placing(flat.shape[1], lax.axis_index("y"))
    return lax.dot_general(
        flat,
        place,
        (((1,), (0,)), ((), ())),
        precision=lax.Precision.HIGHEST,
        preferred_element_type=jnp.float32,
    )


def solution(mesh):
    fine = Mesh(mesh.devices.reshape(Z_HI, Y, CORE, Z_LO, X), DP + MP)
    placed = (
        P(MP, DP, None),
        P(DP, None),
        P(MP, None, None),
        P(MP, None, None),
        P(DP, MP),
    )
    return jax.shard_map(
        shards, mesh=fine, in_specs=placed, out_specs=P(DP + MP, None), check_vma=False
    )
```

time: 147 us -> 100 us (0.68)
  the two profiles are of different devices: /device:TPU:1 before, /device:TPU:25 now
where the time goes in v2:
time: 100 us; the launch traced here: 99.4 us
  starting transfers between devices  59.5 us (60%)
  waiting for transfers between devices  25.1 us (25%)
  matrix products  8.55 us (9%)
  local copies, waits for them, and re-layouts  3.74 us (4%)
  other arithmetic  2.24 us (2%)
    ppermute x9, starting transfers between devices, from_behind(): lax.ppermute(array, axis, [(i, (i + by) % length) for i in range(length)])  30.4 us
    all_to_all x1, starting transfers between devices, shards(): traded = lax.all_to_all(parts, ('core',) + MP, 0, 0, tiled=False)  14.9 us
    all_to_all x1, starting transfers between devices, shards(): lax.all_to_all(copies, 'zh', 0, 0, tiled=False).reshape(Z_HI * EX_DEV, -1)  14.2 us
    all_to_all x1, waiting for transfers between devices, shards(): lax.all_to_all(copies, 'zh', 0, 0, tiled=False).reshape(Z_HI * EX_DEV, -1)  11.7 us
    all_to_all x1, waiting for transfers between devices, shards(): traded = lax.all_to_all(parts, ('core',) + MP, 0, 0, tiled=False)  7.13 us
    ppermute x9, waiting for transfers between devices, from_behind(): lax.ppermute(array, axis, [(i, (i + by) % length) for i in range(length)])  6.28 us
    dot_general x9, matrix products, shards(): lax.dot_general(queries, piece, (((1,), (1,)), ((), ())), preferred_eleme...  5.1 us
  transfers between devices with their start and end apart: 11, of which 7 were waited for; matrix products, arithmetic and copies ran while one was open for 11% of the time, Pallas kernels for 0%

profile of v2, /device:TPU:25, one launch (start us, length us, event | category | flops | bytes accessed | tf_op | source)
XLA Modules:
  0.0 99.4 jit_solution(1706266122550586844)
XLA Ops:
  0.0 2.7 %collective-permute-start = (bf16[96,4096]{1,0:T(8,128)(2,1)}, bf16[96,4096]{1,0:T(8,128)(2,1)S(1)}, u32[]{:S(2)}, u32[]{:S(2)}) collective-permute-start(bf16[96,4096]{1,0:T(8,128)(2,1)} %param.9), channel_id=1, source_target_pairs={{0,12},{12,0},{1,13},{13,1},{2,14},{14,2},{3,15},{15,3},{4,16},{16... | collective-permute-start | bytes 2359304 | tf_op jit(solution)/shard_map/ppermute | solution.py:14
  2.7 0.7 fusion.54
  3.4 0.8 convert_reduce_fusion.1
  4.3 1.1 %slice_bitcast_fusion = bf16[2048,64]{1,0:T(8,128)(2,1)S(1)} fusion(bf16[1,2048,128]{2,1,0:T(8,128)(2,1)} %param.5), kind=kLoop, calls=%fused_computation.84 | loop fusion | bytes 524288 | tf_op jit(solution)/shard_map/mul | solution.py:27
  5.7 0.7 copy-done.1
  6.4 0.9 convolution_bitcast_fusion
  8.3 0.7 broadcast_in_dim.2
  9.0 14.2 %all-to-all-start = ((bf16[4,8,4096]{2,1,0:T(8,128)(2,1)}), bf16[4,8,4096]{2,1,0:T(8,128)(2,1)S(1)}, u32[]{:S(2)}, u32[]{:S(2)}) async-start(bf16[4,8,4096]{2,1,0:T(8,128)(2,1)} %broadcast_in_dim.2), calls=%async_computation | async-start | bytes 524288 | tf_op jit(solution)/shard_map/all_to_all | solution.py:71
  23.3 11.7 %all-to-all-done = bf16[4,8,4096]{2,1,0:T(8,128)(2,1)S(1)} async-done(((bf16[4,8,4096]{2,1,0:T(8,128)(2,1)}), bf16[4,8,4096]{2,1,0:T(8,128)(2,1)S(1)}, u32[]{:S(2)}, u32[]{:S(2)}) %all-to-all-start) | async-done | bytes 262176 | tf_op jit(solution)/shard_map/all_to_all | solution.py:71
  34.9 4.4 %collective-permute-start.1 = (bf16[32,4096]{1,0:T(8,128)(2,1)S(1)}, bf16[32,4096]{1,0:T(8,128)(2,1)S(1)}, u32[]{:S(2)}, u32[]{:S(2)}) collective-permute-start(bf16[32,4096]{1,0:T(8,128)(2,1)S(1)} %bitcast.49), channel_id=1, source_target_pairs={{0,24},{24,48},{48,72},{72,96},{96,120},{120,144},{144,168},{168,0... | collective-permute-start | bytes 786440 | tf_op jit(solution)/shard_map/ppermute | solution.py:14
  39.4 1.9 %collective-permute-start.2 = (bf16[32,4096]{1,0:T(8,128)(2,1)S(1)}, bf16[32,4096]{1,0:T(8,128)(2,1)S(1)}, u32[]{:S(2)}, u32[]{:S(2)}) collective-permute-start(bf16[32,4096]{1,0:T(8,128)(2,1)S(1)} %bitcast.50), channel_id=1, source_target_pairs={{0,168},{24,0},{48,24},{72,48},{96,72},{120,96},{144,120},{168,144... | collective-permute-start | bytes 786440 | tf_op jit(solution)/shard_map/ppermute | solution.py:14
  42.3 1.6 %collective-permute-done.1 = bf16[32,4096]{1,0:T(8,128)(2,1)S(1)} collective-permute-done((bf16[32,4096]{1,0:T(8,128)(2,1)S(1)}, bf16[32,4096]{1,0:T(8,128)(2,1)S(1)}, u32[]{:S(2)}, u32[]{:S(2)}) %collective-permute-start.1) | collective-permute-done | bytes 262176 | tf_op jit(solution)/shard_map/ppermute | solution.py:14
  43.9 5.3 %collective-permute-start.3 = (bf16[32,4096]{1,0:T(8,128)(2,1)S(1)}, bf16[32,4096]{1,0:T(8,128)(2,1)S(1)}, u32[]{:S(2)}, u32[]{:S(2)}) collective-permute-start(bf16[32,4096]{1,0:T(8,128)(2,1)S(1)} %collective-permute-done.1), channel_id=1, source_target_pairs={{0,24},{24,48},{48,72},{72,96},{96,120},{120,144},{144,168},{168,0... | collective-permute-start | bytes 786440 | tf_op jit(solution)/shard_map/ppermute | solution.py:14
  49.8 1.9 %collective-permute-start.4 = (bf16[32,4096]{1,0:T(8,128)(2,1)S(1)}, bf16[32,4096]{1,0:T(8,128)(2,1)S(1)}, u32[]{:S(2)}, u32[]{:S(2)}) collective-permute-start(bf16[32,4096]{1,0:T(8,128)(2,1)S(1)} %collective-permute-done.2), channel_id=1, source_target_pairs={{0,168},{24,0},{48,24},{72,48},{96,72},{120,96},{144,120},{168,144... | collective-permute-start | bytes 786440 | tf_op jit(solution)/shard_map/ppermute | solution.py:14
  52.9 5.3 %collective-permute-start.5 = (bf16[32,4096]{1,0:T(8,128)(2,1)S(1)}, bf16[32,4096]{1,0:T(8,128)(2,1)S(1)}, u32[]{:S(2)}, u32[]{:S(2)}) collective-permute-start(bf16[32,4096]{1,0:T(8,128)(2,1)S(1)} %collective-permute-done.3), channel_id=1, source_target_pairs={{0,24},{24,48},{48,72},{72,96},{96,120},{120,144},{144,168},{168,0... | collective-permute-start | bytes 786440 | tf_op jit(solution)/shard_map/ppermute | solution.py:14
  58.8 1.9 %collective-permute-start.6 = (bf16[32,4096]{1,0:T(8,128)(2,1)S(1)}, bf16[32,4096]{1,0:T(8,128)(2,1)S(1)}, u32[]{:S(2)}, u32[]{:S(2)}) collective-permute-start(bf16[32,4096]{1,0:T(8,128)(2,1)S(1)} %collective-permute-done.4), channel_id=1, source_target_pairs={{0,168},{24,0},{48,24},{72,48},{96,72},{120,96},{144,120},{168,144... | collective-permute-start | bytes 786440 | tf_op jit(solution)/shard_map/ppermute | solution.py:14
  61.5 5.0 %collective-permute-start.7 = (bf16[16,4096]{1,0:T(8,128)(2,1)S(1)}, bf16[16,4096]{1,0:T(8,128)(2,1)S(1)}, u32[]{:S(2)}, u32[]{:S(2)}) collective-permute-start(bf16[16,4096]{1,0:T(8,128)(2,1)S(1)} %slice.24), channel_id=1, source_target_pairs={{0,24},{24,48},{48,72},{72,96},{96,120},{120,144},{144,168},{168,0... | collective-permute-start | bytes 393224 | tf_op jit(solution)/shard_map/ppermute | solution.py:14
  67.2 1.9 %collective-permute-start.8 = (bf16[16,4096]{1,0:T(8,128)(2,1)S(1)}, bf16[16,4096]{1,0:T(8,128)(2,1)S(1)}, u32[]{:S(2)}, u32[]{:S(2)}) collective-permute-start(bf16[16,4096]{1,0:T(8,128)(2,1)S(1)} %slice.25), channel_id=1, source_target_pairs={{0,168},{24,0},{48,24},{72,48},{96,72},{120,96},{144,120},{168,144... | collective-permute-start | bytes 393224 | tf_op jit(solution)/shard_map/ppermute | solution.py:14
  69.7 0.6 fusion
  70.8 3.3 %collective-permute-done.8 = bf16[16,4096]{1,0:T(8,128)(2,1)S(1)} collective-permute-done((bf16[16,4096]{1,0:T(8,128)(2,1)S(1)}, bf16[16,4096]{1,0:T(8,128)(2,1)S(1)}, u32[]{:S(2)}, u32[]{:S(2)}) %collective-permute-start.8) | collective-permute-done | bytes 131104 | tf_op jit(solution)/shard_map/ppermute | solution.py:14
  74.6 0.8 copy.7
  75.4 14.9 %all-to-all-start.1 = ((bf16[24,8,256]{2,1,0:T(8,128)(2,1)}), bf16[24,8,256]{2,1,0:T(8,128)(2,1)S(1)}, u32[]{:S(2)}, u32[]{:S(2)}) async-start(bf16[24,8,256]{2,1,0:T(8,128)(2,1)} %bitcast.11), calls=%async_computation.1 | async-start | bytes 196608 | tf_op jit(solution)/shard_map/all_to_all | solution.py:90
  90.3 7.1 %all-to-all-done.1 = bf16[24,8,256]{2,1,0:T(8,128)(2,1)S(1)} async-done(((bf16[24,8,256]{2,1,0:T(8,128)(2,1)}), bf16[24,8,256]{2,1,0:T(8,128)(2,1)S(1)}, u32[]{:S(2)}, u32[]{:S(2)}) %all-to-all-start.1) | async-done | bytes 98336 | tf_op jit(solution)/shard_map/all_to_all | solution.py:90
  97.4 2.0 %fusion.27 = f32[8,512]{1,0:T(8,128)} fusion(s32[512]{0:T(512)S(1)} %get-tuple-element.8, s32[512]{0:T(512)S(1)} %get-tuple-element.11, s32[512]{0:T(512)S(1)} %get-tuple-element.9, s32[512]{0:T(512)S(1)} %get-tuple-element.12, s32[512]{0:T(512)S(1)} %get-tuple-element.10, s32[512]{0:T(512)S(1)} %get-tuple-element.17, s32[]{:T(128)S(6)} %axis_index.28, ...), kind=kOutput, calls=%fused_computation.64 | convolution fusion | flops 46927872 | bytes 51204 | tf_op jit(solution)/shard_map/dot_general | solution.py:96
  (40 shorter events, 7.6 us)
Async XLA Ops:
  0.0 7.5 %copy-start = (bf16[1,64,64]{2,1,0:T(8,128)(2,1)S(1)}, bf16[1,64,64]{2,1,0:T(8,128)(2,1)}, u32[]{:S(2)}) copy-start(bf16[1,64,64]{2,1,0:T(8,128)(2,1)} %param.7) | copy-start | bytes 24580
  0.0 41.3 %collective-permute-start = (bf16[96,4096]{1,0:T(8,128)(2,1)}, bf16[96,4096]{1,0:T(8,128)(2,1)S(1)}, u32[]{:S(2)}, u32[]{:S(2)}) collective-permute-start(bf16[96,4096]{1,0:T(8,128)(2,1)} %param.9), channel_id=1, source_target_pairs={{0,12},{12,0},{1,13},{13,1},{2,14},{14,2},{3,15},{15,3},{4,16},{16... | collective-permute-start | bytes 2359304 | tf_op jit(solution)/shard_map/ppermute | solution.py:14
  5.3 1.0 %copy-start.1 = (bf16[1,2048,128]{2,1,0:T(8,128)(2,1)S(1)}, bf16[1,2048,128]{2,1,0:T(8,128)(2,1)}, u32[]{:S(2)}) copy-start(bf16[1,2048,128]{2,1,0:T(8,128)(2,1)} %param.5) | copy-start | bytes 1572868
  6.4 1.5 %copy-start.3 = (bf16[1,64,64]{2,1,0:T(8,128)(2,1)S(1)}, bf16[1,64,64]{2,1,0:T(8,128)(2,1)}, u32[]{:S(2)}) copy-start(bf16[1,64,64]{2,1,0:T(8,128)(2,1)} %param.8) | copy-start | bytes 24580
  7.3 34.0 %copy-start.2 = (bf16[96,4096]{1,0:T(8,128)(2,1)S(1)}, bf16[96,4096]{1,0:T(8,128)(2,1)}, u32[]{:S(2)}) copy-start(bf16[96,4096]{1,0:T(8,128)(2,1)} %param.9) | copy-start | bytes 2359300
  9.0 25.9 %all-to-all-start = ((bf16[4,8,4096]{2,1,0:T(8,128)(2,1)}), bf16[4,8,4096]{2,1,0:T(8,128)(2,1)S(1)}, u32[]{:S(2)}, u32[]{:S(2)}) async-start(bf16[4,8,4096]{2,1,0:T(8,128)(2,1)} %broadcast_in_dim.2), calls=%async_computation | async-start | bytes 524288 | tf_op jit(solution)/shard_map/all_to_all | solution.py:71
  34.9 9.0 %collective-permute-start.1 = (bf16[32,4096]{1,0:T(8,128)(2,1)S(1)}, bf16[32,4096]{1,0:T(8,128)(2,1)S(1)}, u32[]{:S(2)}, u32[]{:S(2)}) collective-permute-start(bf16[32,4096]{1,0:T(8,128)(2,1)S(1)} %bitcast.49), channel_id=1, source_target_pairs={{0,24},{24,48},{48,72},{72,96},{96,120},{120,144},{144,168},{168,0... | collective-permute-start | bytes 786440 | tf_op jit(solution)/shard_map/ppermute | solution.py:14
  39.4 10.5 %collective-permute-start.2 = (bf16[32,4096]{1,0:T(8,128)(2,1)S(1)}, bf16[32,4096]{1,0:T(8,128)(2,1)S(1)}, u32[]{:S(2)}, u32[]{:S(2)}) collective-permute-start(bf16[32,4096]{1,0:T(8,128)(2,1)S(1)} %bitcast.50), channel_id=1, source_target_pairs={{0,168},{24,0},{48,24},{72,48},{96,72},{120,96},{144,120},{168,144... | collective-permute-start | bytes 786440 | tf_op jit(solution)/shard_map/ppermute | solution.py:14
  43.9 9.0 %collective-permute-start.3 = (bf16[32,4096]{1,0:T(8,128)(2,1)S(1)}, bf16[32,4096]{1,0:T(8,128)(2,1)S(1)}, u32[]{:S(2)}, u32[]{:S(2)}) collective-permute-start(bf16[32,4096]{1,0:T(8,128)(2,1)S(1)} %collective-permute-done.1), channel_id=1, source_target_pairs={{0,24},{24,48},{48,72},{72,96},{96,120},{120,144},{144,168},{168,0... | collective-permute-start | bytes 786440 | tf_op jit(solution)/shard_map/ppermute | solution.py:14
  49.8 9.0 %collective-permute-start.4 = (bf16[32,4096]{1,0:T(8,128)(2,1)S(1)}, bf16[32,4096]{1,0:T(8,128)(2,1)S(1)}, u32[]{:S(2)}, u32[]{:S(2)}) collective-permute-start(bf16[32,4096]{1,0:T(8,128)(2,1)S(1)} %collective-permute-done.2), channel_id=1, source_target_pairs={{0,168},{24,0},{48,24},{72,48},{96,72},{120,96},{144,120},{168,144... | collective-permute-start | bytes 786440 | tf_op jit(solution)/shard_map/ppermute | solution.py:14
  52.9 8.6 %collective-permute-start.5 = (bf16[32,4096]{1,0:T(8,128)(2,1)S(1)}, bf16[32,4096]{1,0:T(8,128)(2,1)S(1)}, u32[]{:S(2)}, u32[]{:S(2)}) collective-permute-start(bf16[32,4096]{1,0:T(8,128)(2,1)S(1)} %collective-permute-done.3), channel_id=1, source_target_pairs={{0,24},{24,48},{48,72},{72,96},{96,120},{120,144},{144,168},{168,0... | collective-permute-start | bytes 786440 | tf_op jit(solution)/shard_map/ppermute | solution.py:14
  58.8 8.3 %collective-permute-start.6 = (bf16[32,4096]{1,0:T(8,128)(2,1)S(1)}, bf16[32,4096]{1,0:T(8,128)(2,1)S(1)}, u32[]{:S(2)}, u32[]{:S(2)}) collective-permute-start(bf16[32,4096]{1,0:T(8,128)(2,1)S(1)} %collective-permute-done.4), channel_id=1, source_target_pairs={{0,168},{24,0},{48,24},{72,48},{96,72},{120,96},{144,120},{168,144... | collective-permute-start | bytes 786440 | tf_op jit(solution)/shard_map/ppermute | solution.py:14
  61.5 8.8 %collective-permute-start.7 = (bf16[16,4096]{1,0:T(8,128)(2,1)S(1)}, bf16[16,4096]{1,0:T(8,128)(2,1)S(1)}, u32[]{:S(2)}, u32[]{:S(2)}) collective-permute-start(bf16[16,4096]{1,0:T(8,128)(2,1)S(1)} %slice.24), channel_id=1, source_target_pairs={{0,24},{24,48},{48,72},{72,96},{96,120},{120,144},{144,168},{168,0... | collective-permute-start | bytes 393224 | tf_op jit(solution)/shard_map/ppermute | solution.py:14
  67.2 6.9 %collective-permute-start.8 = (bf16[16,4096]{1,0:T(8,128)(2,1)S(1)}, bf16[16,4096]{1,0:T(8,128)(2,1)S(1)}, u32[]{:S(2)}, u32[]{:S(2)}) collective-permute-start(bf16[16,4096]{1,0:T(8,128)(2,1)S(1)} %slice.25), channel_id=1, source_target_pairs={{0,168},{24,0},{48,24},{72,48},{96,72},{120,96},{144,120},{168,144... | collective-permute-start | bytes 393224 | tf_op jit(solution)/shard_map/ppermute | solution.py:14
  75.4 22.1 %all-to-all-start.1 = ((bf16[24,8,256]{2,1,0:T(8,128)(2,1)}), bf16[24,8,256]{2,1,0:T(8,128)(2,1)S(1)}, u32[]{:S(2)}, u32[]{:S(2)}) async-start(bf16[24,8,256]{2,1,0:T(8,128)(2,1)} %bitcast.11), calls=%async_computation.1 | async-start | bytes 196608 | tf_op jit(solution)/shard_map/all_to_all | solution.py:90

commit v3 on v2

v3 whole, which is shorter than its diff:
```python
import jax
import jax.numpy as jnp
from jax import lax
from jax.sharding import Mesh, PartitionSpec as P

EX_DEV = 8
Z_HI, Y, CORE, Z_LO, X = 4, 8, 2, 3, 4
DP = ("zh", "y", "core")
MP = ("zl", "x")


def from_behind(array, axis, by):
    length = lax.axis_size(axis)
    return lax.ppermute(array, axis, [(i, (i + by) % length) for i in range(length)])


def onward(array):
    steps = [
        ((i, core), ((i + (1 if core == 0 else Y - 1)) % Y, core)) for i in range(Y) for core in range(CORE)
    ]
    flat = [(a[0] * CORE + a[1], b[0] * CORE + b[1]) for a, b in steps]
    return lax.ppermute(array, ("y", "core"), flat)


def block_features(token_factors, example_ids, left_factor, right_factor):
    proj_rank = left_factor.shape[1]
    tokens_here = token_factors.shape[1]
    examples = EX_DEV
    labels = example_ids[0]
    onehot = labels[:, None] == jnp.arange(examples, dtype=jnp.int32)[None, :]
    selector = onehot.astype(jnp.bfloat16)
    counts = jnp.sum(onehot.astype(jnp.float32), axis=0)
    inputs = token_factors[0, :, :proj_rank]
    outputs = token_factors[0, :, proj_rank:]
    masked = (selector[:, :, None] * inputs[:, None, :]).reshape(tokens_here, examples * proj_rank)
    summed = lax.dot_general(
        outputs, masked, (((0,), (0,)), ((), ())), preferred_element_type=jnp.float32
    )
    gradient = (
        summed.reshape(proj_rank, examples, proj_rank).transpose(1, 0, 2) / counts[:, None, None]
    )
    precond = jnp.einsum(
        "ac,ecd,db->eab",
        left_factor[0].astype(jnp.float32),
        gradient,
        right_factor[0].astype(jnp.float32),
        precision=lax.Precision.HIGHEST,
    )
    return precond.reshape(examples, proj_rank * proj_rank).astype(jnp.bfloat16)


def both_cores(mine, partner, core):
    return jnp.where(
        core == 0,
        jnp.concatenate([mine, partner], axis=0),
        jnp.concatenate([partner, mine], axis=0),
    )


def placing(width, y):
    source = lax.broadcasted_iota(jnp.int32, (width, width), 0)
    result = lax.broadcasted_iota(jnp.int32, (width, width), 1)
    example = source % EX_DEV
    z_hi = source // EX_DEV % Z_HI
    piece = source // (EX_DEV * Z_HI) % Y
    core = source // (EX_DEV * Z_HI * Y)
    away = (piece + 1) // 2
    from_y = (y + jnp.where(core == 0, Y - away, away)) % Y
    from_core = jnp.where((piece % 2 == 1) | (piece == 0), core, 1 - core)
    return (result == ((z_hi * Y + from_y) * CORE + from_core) * EX_DEV + example).astype(
        jnp.bfloat16
    )


def to_all(array, axis):
    copies = jnp.broadcast_to(array[None], (lax.axis_size(axis),) + array.shape)
    return lax.all_to_all(copies, axis, 0, 0, tiled=False)


def scored(queries, pieces):
    return lax.dot_general(
        queries, pieces, (((1,), (1,)), ((), ())), preferred_element_type=jnp.float32
    )


def shards(token_factors, example_ids, left_factor, right_factor, query_features):
    rows, width = query_features.shape
    y, core = lax.axis_index("y"), lax.axis_index("core")
    features = block_features(token_factors, example_ids, left_factor, right_factor)
    features, query_features = lax.optimization_barrier((features, query_features))

    mine = to_all(features, "zh").reshape(Z_HI * EX_DEV, width)
    other = from_behind(query_features, "core", 1)
    queries = both_cores(query_features, other, core)
    place = placing(CORE * Y * Z_HI * EX_DEV, y)
    mine, place = lax.optimization_barrier((mine, place))

    partner = from_behind(mine, "core", 1)
    pieces = [mine]
    for step in range(1, Y // 2 + 1):
        mine = onward(mine)
        pieces.append(mine)
        if step < Y // 2:
            partner = onward(partner)
            pieces.append(partner)

    scores = [scored(queries, piece) for piece in pieces]
    members = Z_LO * X
    parts = jnp.concatenate([part.astype(jnp.bfloat16) for part in scores], axis=1)
    parts = parts.reshape(CORE * members, rows // members, -1)
    traded = lax.all_to_all(parts, ("core",) + MP, 0, 0, tiled=False).reshape(CORE, rows, -1)
    placed = sum(
        lax.dot_general(
            traded[i],
            place[i * traded.shape[2] : (i + 1) * traded.shape[2]],
            (((1,), (0,)), ((), ())),
            preferred_element_type=jnp.float32,
        )
        for i in range(CORE)
    )
    return jnp.sum(placed.reshape(members, rows // members, -1), axis=0)


def solution(mesh):
    fine = Mesh(mesh.devices.reshape(Z_HI, Y, CORE, Z_LO, X), DP + MP)
    placed = (
        P(MP, DP, None),
        P(DP, None),
        P(MP, None, None),
        P(MP, None, None),
        P(DP, MP),
    )
    return jax.shard_map(
        shards, mesh=fine, in_specs=placed, out_specs=P(DP + MP, None), check_vma=False
    )
```

time: 100 us -> 91.7 us (0.917)
  the two profiles are of different devices: /device:TPU:25 before, /device:TPU:1 now
where the time goes in v3:
time: 91.7 us; the launch traced here: 91 us
  starting transfers between devices  50.2 us (55%)
  blocking collectives  17 us (19%)
  waiting for transfers between devices  9.87 us (11%)
  matrix products  7.09 us (8%)
  other arithmetic  3.54 us (4%)
  local copies, waits for them, and re-layouts  3.06 us (3%)
    ppermute x7, starting transfers between devices, onward(): return lax.ppermute(array, ('y', 'core'), flat)  26.4 us
    all_to_all x1, blocking collectives, shards(): lax.all_to_all(parts, ('core',) + MP, 0, 0, tiled=False)  17 us
    all_to_all x1, starting transfers between devices, to_all(): return lax.all_to_all(copies, axis, 0, 0, tiled=False)  15 us
    ppermute x2, starting transfers between devices, from_behind(): lax.ppermute(array, axis, [(i, (i + by) % length) for i in range(length)])  8.69 us
    all_to_all x1, waiting for transfers between devices, to_all(): return lax.all_to_all(copies, axis, 0, 0, tiled=False)  6.47 us
    dot_general x8, matrix products, scored(): lax.dot_general(queries, pieces, (((1,), (1,)), ((), ())), preferred_elem...  4.64 us
    ppermute x7, waiting for transfers between devices, onward(): return lax.ppermute(array, ('y', 'core'), flat)  3.25 us
  transfers between devices with their start and end apart: 10, of which 3 were waited for; matrix products, arithmetic and copies ran while one was open for 6% of the time, Pallas kernels for 0%

profile of v3, /device:TPU:1, one launch (start us, length us, event | category | flops | bytes accessed | tf_op | source)
XLA Modules:
  0.0 91.0 jit_solution(10855271983260287583)
XLA Ops:
  0.0 0.7 fusion.35
  0.7 0.8 convert_reduce_fusion
  1.6 1.1 %slice_bitcast_fusion = bf16[2048,64]{1,0:T(8,128)(2,1)S(1)} fusion(bf16[1,2048,128]{2,1,0:T(8,128)(2,1)} %param.5), kind=kLoop, calls=%fused_computation.68 | loop fusion | bytes 524288 | tf_op jit(solution)/shard_map/mul | solution.py:35
  3.0 0.7 copy-done.1
  3.7 0.9 %convolution_bitcast_fusion = f32[64,512]{1,0:T(8,128)S(1)} fusion(bf16[2048,512]{0,1:T(8,128)(2,1)S(1)} %bitcast.49, bf16[1,2048,128]{2,1,0:T(8,128)(2,1)S(1)} %copy-done.1), kind=kOutput, calls=%fused_computation.28 | convolution fusion | flops 134217728 | bytes 2752512 | tf_op jit(solution)/shard_map/dot_general | solution.py:36
  5.6 0.7 broadcast_in_dim.2
  6.3 15.0 %all-to-all-start = ((bf16[4,8,4096]{2,1,0:T(8,128)(2,1)}), bf16[4,8,4096]{2,1,0:T(8,128)(2,1)S(1)}, u32[]{:S(2)}, u32[]{:S(2)}) async-start(bf16[4,8,4096]{2,1,0:T(8,128)(2,1)} %broadcast_in_dim.2), calls=%async_computation | async-start | bytes 524288 | tf_op jit(solution)/shard_map/all_to_all | solution.py:77
  21.4 2.9 %collective-permute-start = (bf16[96,4096]{1,0:T(8,128)(2,1)S(1)}, bf16[96,4096]{1,0:T(8,128)(2,1)S(1)}, u32[]{:S(2)}, u32[]{:S(2)}) collective-permute-start(bf16[96,4096]{1,0:T(8,128)(2,1)S(1)} %copy-done.2), channel_id=1, source_target_pairs={{0,12},{12,0},{1,13},{13,1},{2,14},{14,2},{3,15},{15,3},{4,16},{16... | collective-permute-start | bytes 2359304 | tf_op jit(solution)/shard_map/ppermute | solution.py:14
  24.3 1.3 %fusion.27 = bf16[512,512]{1,0:T(8,128)(2,1)S(1)} fusion(s32[512]{0:T(512)S(1)} %get-tuple-element.16, s32[512]{0:T(512)S(1)} %get-tuple-element.17, s32[512]{0:T(512)S(1)} %get-tuple-element.13, s32[512]{0:T(512)S(1)} %get-tuple-element.18, s32[512]{0:T(512)S(1)} %get-tuple-element.14, s32[512]{0:T(512)S(1)} %get-tuple-element.23, s32[]{:T(128)S(6)} %axis_index.28, ...), kind=kLoop, calls=%fused_computation.65 | loop fusion | flops 21233664 | bytes 542724 | tf_op jit(solution)/shard_map/convert_element_type | solution.py:70
  25.6 6.5 %all-to-all-done = bf16[4,8,4096]{2,1,0:T(8,128)(2,1)S(1)} async-done(((bf16[4,8,4096]{2,1,0:T(8,128)(2,1)}), bf16[4,8,4096]{2,1,0:T(8,128)(2,1)S(1)}, u32[]{:S(2)}, u32[]{:S(2)}) %all-to-all-start) | async-done | bytes 262176 | tf_op jit(solution)/shard_map/all_to_all | solution.py:77
  32.1 5.1 %collective-permute-start.1 = (bf16[32,4096]{1,0:T(8,128)(2,1)S(1)}, bf16[32,4096]{1,0:T(8,128)(2,1)S(1)}, u32[]{:S(2)}, u32[]{:S(2)}) collective-permute-start(bf16[32,4096]{1,0:T(8,128)(2,1)S(1)} %bitcast.50), channel_id=1, source_target_pairs={{0,24},{12,180},{24,48},{36,12},{48,72},{60,36},{72,96},{84,60},{9... | collective-permute-start | bytes 786440 | tf_op jit(solution)/shard_map/ppermute | solution.py:22
  37.2 5.8 %collective-permute-start.2 = (bf16[32,4096]{1,0:T(8,128)(2,1)S(1)}, bf16[32,4096]{1,0:T(8,128)(2,1)S(1)}, u32[]{:S(2)}, u32[]{:S(2)}) collective-permute-start(bf16[32,4096]{1,0:T(8,128)(2,1)S(1)} %bitcast.51), channel_id=1, source_target_pairs={{0,12},{12,0},{1,13},{13,1},{2,14},{14,2},{3,15},{15,3},{4,16},{16... | collective-permute-start | bytes 786440 | tf_op jit(solution)/shard_map/ppermute | solution.py:14
  43.4 0.6 fusion.9
  44.2 3.5 %collective-permute-start.3 = (bf16[32,4096]{1,0:T(8,128)(2,1)S(1)}, bf16[32,4096]{1,0:T(8,128)(2,1)S(1)}, u32[]{:S(2)}, u32[]{:S(2)}) collective-permute-start(bf16[32,4096]{1,0:T(8,128)(2,1)S(1)} %collective-permute-done.2), channel_id=1, source_target_pairs={{0,24},{12,180},{24,48},{36,12},{48,72},{60,36},{72,96},{84,60},{9... | collective-permute-start | bytes 786440 | tf_op jit(solution)/shard_map/ppermute | solution.py:22
  47.7 3.6 %collective-permute-start.4 = (bf16[32,4096]{1,0:T(8,128)(2,1)S(1)}, bf16[32,4096]{1,0:T(8,128)(2,1)S(1)}, u32[]{:S(2)}, u32[]{:S(2)}) collective-permute-start(bf16[32,4096]{1,0:T(8,128)(2,1)S(1)} %collective-permute-done.1), channel_id=1, source_target_pairs={{0,24},{12,180},{24,48},{36,12},{48,72},{60,36},{72,96},{84,60},{9... | collective-permute-start | bytes 786440 | tf_op jit(solution)/shard_map/ppermute | solution.py:22
  52.0 4.0 %collective-permute-start.5 = (bf16[32,4096]{1,0:T(8,128)(2,1)S(1)}, bf16[32,4096]{1,0:T(8,128)(2,1)S(1)}, u32[]{:S(2)}, u32[]{:S(2)}) collective-permute-start(bf16[32,4096]{1,0:T(8,128)(2,1)S(1)} %collective-permute-done.3), channel_id=1, source_target_pairs={{0,24},{12,180},{24,48},{36,12},{48,72},{60,36},{72,96},{84,60},{9... | collective-permute-start | bytes 786440 | tf_op jit(solution)/shard_map/ppermute | solution.py:22
  56.0 0.6 fusion.7
  56.6 3.0 %collective-permute-start.6 = (bf16[32,4096]{1,0:T(8,128)(2,1)S(1)}, bf16[32,4096]{1,0:T(8,128)(2,1)S(1)}, u32[]{:S(2)}, u32[]{:S(2)}) collective-permute-start(bf16[32,4096]{1,0:T(8,128)(2,1)S(1)} %collective-permute-done.4), channel_id=1, source_target_pairs={{0,24},{12,180},{24,48},{36,12},{48,72},{60,36},{72,96},{84,60},{9... | collective-permute-start | bytes 786440 | tf_op jit(solution)/shard_map/ppermute | solution.py:22
  59.7 0.6 fusion.6
  60.3 4.0 %collective-permute-start.7 = (bf16[32,4096]{1,0:T(8,128)(2,1)S(1)}, bf16[32,4096]{1,0:T(8,128)(2,1)S(1)}, u32[]{:S(2)}, u32[]{:S(2)}) collective-permute-start(bf16[32,4096]{1,0:T(8,128)(2,1)S(1)} %collective-permute-done.5), channel_id=1, source_target_pairs={{0,24},{12,180},{24,48},{36,12},{48,72},{60,36},{72,96},{84,60},{9... | collective-permute-start | bytes 786440 | tf_op jit(solution)/shard_map/ppermute | solution.py:22
  64.9 3.0 %collective-permute-start.8 = (bf16[32,4096]{1,0:T(8,128)(2,1)S(1)}, bf16[32,4096]{1,0:T(8,128)(2,1)S(1)}, u32[]{:S(2)}, u32[]{:S(2)}) collective-permute-start(bf16[32,4096]{1,0:T(8,128)(2,1)S(1)} %collective-permute-done.6), channel_id=1, source_target_pairs={{0,24},{12,180},{24,48},{36,12},{48,72},{60,36},{72,96},{84,60},{9... | collective-permute-start | bytes 786440 | tf_op jit(solution)/shard_map/ppermute | solution.py:22
  69.2 3.2 %collective-permute-done.8 = bf16[32,4096]{1,0:T(8,128)(2,1)S(1)} collective-permute-done((bf16[32,4096]{1,0:T(8,128)(2,1)S(1)}, bf16[32,4096]{1,0:T(8,128)(2,1)S(1)}, u32[]{:S(2)}, u32[]{:S(2)}) %collective-permute-start.8) | collective-permute-done | bytes 262176 | tf_op jit(solution)/shard_map/ppermute | solution.py:22
  73.0 17.0 %all_to_all.10 = bf16[24,8,256]{2,1,0:T(8,128)(2,1)S(1)} all-to-all(bf16[24,8,256]{2,1,0:T(8,128)(2,1)S(1)} %bitcast.53), channel_id=1, replica_groups=mesh['zh'=4,'y'=8,'core'=2,'zl'=3,'x'=4] {'core','zl','x'}, dimensions={0} | all-to-all | bytes 196608 | tf_op jit(solution)/shard_map/all_to_all | solution.py:111
  90.2 0.8 fusion.1
  (36 shorter events, 5.1 us)
Async XLA Ops:
  0.0 4.8 %copy-start = (bf16[1,64,64]{2,1,0:T(8,128)(2,1)S(1)}, bf16[1,64,64]{2,1,0:T(8,128)(2,1)}, u32[]{:S(2)}) copy-start(bf16[1,64,64]{2,1,0:T(8,128)(2,1)} %param.7) | copy-start | bytes 24580
  2.6 1.0 %copy-start.1 = (bf16[1,2048,128]{2,1,0:T(8,128)(2,1)S(1)}, bf16[1,2048,128]{2,1,0:T(8,128)(2,1)}, u32[]{:S(2)}) copy-start(bf16[1,2048,128]{2,1,0:T(8,128)(2,1)} %param.5) | copy-start | bytes 1572868
  3.7 1.5 %copy-start.3 = (bf16[1,64,64]{2,1,0:T(8,128)(2,1)S(1)}, bf16[1,64,64]{2,1,0:T(8,128)(2,1)}, u32[]{:S(2)}) copy-start(bf16[1,64,64]{2,1,0:T(8,128)(2,1)} %param.8) | copy-start | bytes 24580
  4.6 16.7 %copy-start.2 = (bf16[96,4096]{1,0:T(8,128)(2,1)S(1)}, bf16[96,4096]{1,0:T(8,128)(2,1)}, u32[]{:S(2)}) copy-start(bf16[96,4096]{1,0:T(8,128)(2,1)} %param.9) | copy-start | bytes 2359300
  6.3 25.8 %all-to-all-start = ((bf16[4,8,4096]{2,1,0:T(8,128)(2,1)}), bf16[4,8,4096]{2,1,0:T(8,128)(2,1)S(1)}, u32[]{:S(2)}, u32[]{:S(2)}) async-start(bf16[4,8,4096]{2,1,0:T(8,128)(2,1)} %broadcast_in_dim.2), calls=%async_computation | async-start | bytes 524288 | tf_op jit(solution)/shard_map/all_to_all | solution.py:77
  21.4 21.7 %collective-permute-start = (bf16[96,4096]{1,0:T(8,128)(2,1)S(1)}, bf16[96,4096]{1,0:T(8,128)(2,1)S(1)}, u32[]{:S(2)}, u32[]{:S(2)}) collective-permute-start(bf16[96,4096]{1,0:T(8,128)(2,1)S(1)} %copy-done.2), channel_id=1, source_target_pairs={{0,12},{12,0},{1,13},{13,1},{2,14},{14,2},{3,15},{15,3},{4,16},{16... | collective-permute-start | bytes 2359304 | tf_op jit(solution)/shard_map/ppermute | solution.py:14
  32.1 15.6 %collective-permute-start.1 = (bf16[32,4096]{1,0:T(8,128)(2,1)S(1)}, bf16[32,4096]{1,0:T(8,128)(2,1)S(1)}, u32[]{:S(2)}, u32[]{:S(2)}) collective-permute-start(bf16[32,4096]{1,0:T(8,128)(2,1)S(1)} %bitcast.50), channel_id=1, source_target_pairs={{0,24},{12,180},{24,48},{36,12},{48,72},{60,36},{72,96},{84,60},{9... | collective-permute-start | bytes 786440 | tf_op jit(solution)/shard_map/ppermute | solution.py:22
  37.2 7.0 %collective-permute-start.2 = (bf16[32,4096]{1,0:T(8,128)(2,1)S(1)}, bf16[32,4096]{1,0:T(8,128)(2,1)S(1)}, u32[]{:S(2)}, u32[]{:S(2)}) collective-permute-start(bf16[32,4096]{1,0:T(8,128)(2,1)S(1)} %bitcast.51), channel_id=1, source_target_pairs={{0,12},{12,0},{1,13},{13,1},{2,14},{14,2},{3,15},{15,3},{4,16},{16... | collective-permute-start | bytes 786440 | tf_op jit(solution)/shard_map/ppermute | solution.py:14
  44.2 7.8 %collective-permute-start.3 = (bf16[32,4096]{1,0:T(8,128)(2,1)S(1)}, bf16[32,4096]{1,0:T(8,128)(2,1)S(1)}, u32[]{:S(2)}, u32[]{:S(2)}) collective-permute-start(bf16[32,4096]{1,0:T(8,128)(2,1)S(1)} %collective-permute-done.2), channel_id=1, source_target_pairs={{0,24},{12,180},{24,48},{36,12},{48,72},{60,36},{72,96},{84,60},{9... | collective-permute-start | bytes 786440 | tf_op jit(solution)/shard_map/ppermute | solution.py:22
  47.7 8.9 %collective-permute-start.4 = (bf16[32,4096]{1,0:T(8,128)(2,1)S(1)}, bf16[32,4096]{1,0:T(8,128)(2,1)S(1)}, u32[]{:S(2)}, u32[]{:S(2)}) collective-permute-start(bf16[32,4096]{1,0:T(8,128)(2,1)S(1)} %collective-permute-done.1), channel_id=1, source_target_pairs={{0,24},{12,180},{24,48},{36,12},{48,72},{60,36},{72,96},{84,60},{9... | collective-permute-start | bytes 786440 | tf_op jit(solution)/shard_map/ppermute | solution.py:22
  52.0 8.3 %collective-permute-start.5 = (bf16[32,4096]{1,0:T(8,128)(2,1)S(1)}, bf16[32,4096]{1,0:T(8,128)(2,1)S(1)}, u32[]{:S(2)}, u32[]{:S(2)}) collective-permute-start(bf16[32,4096]{1,0:T(8,128)(2,1)S(1)} %collective-permute-done.3), channel_id=1, source_target_pairs={{0,24},{12,180},{24,48},{36,12},{48,72},{60,36},{72,96},{84,60},{9... | collective-permute-start | bytes 786440 | tf_op jit(solution)/shard_map/ppermute | solution.py:22
  56.6 8.3 %collective-permute-start.6 = (bf16[32,4096]{1,0:T(8,128)(2,1)S(1)}, bf16[32,4096]{1,0:T(8,128)(2,1)S(1)}, u32[]{:S(2)}, u32[]{:S(2)}) collective-permute-start(bf16[32,4096]{1,0:T(8,128)(2,1)S(1)} %collective-permute-done.4), channel_id=1, source_target_pairs={{0,24},{12,180},{24,48},{36,12},{48,72},{60,36},{72,96},{84,60},{9... | collective-permute-start | bytes 786440 | tf_op jit(solution)/shard_map/ppermute | solution.py:22
  60.3 8.3 %collective-permute-start.7 = (bf16[32,4096]{1,0:T(8,128)(2,1)S(1)}, bf16[32,4096]{1,0:T(8,128)(2,1)S(1)}, u32[]{:S(2)}, u32[]{:S(2)}) collective-permute-start(bf16[32,4096]{1,0:T(8,128)(2,1)S(1)} %collective-permute-done.5), channel_id=1, source_target_pairs={{0,24},{12,180},{24,48},{36,12},{48,72},{60,36},{72,96},{84,60},{9... | collective-permute-start | bytes 786440 | tf_op jit(solution)/shard_map/ppermute | solution.py:22
  64.9 7.4 %collective-permute-start.8 = (bf16[32,4096]{1,0:T(8,128)(2,1)S(1)}, bf16[32,4096]{1,0:T(8,128)(2,1)S(1)}, u32[]{:S(2)}, u32[]{:S(2)}) collective-permute-start(bf16[32,4096]{1,0:T(8,128)(2,1)S(1)} %collective-permute-done.6), channel_id=1, source_target_pairs={{0,24},{12,180},{24,48},{36,12},{48,72},{60,36},{72,96},{84,60},{9... | collective-permute-start | bytes 786440 | tf_op jit(solution)/shard_map/ppermute | solution.py:22

commit v4 on v3

--- a/solution.py
+++ b/solution.py
@@ -1,6 +1,8 @@
 import jax
 import jax.numpy as jnp
 from jax import lax
+from jax.experimental import pallas as pl
+from jax.experimental.pallas import tpu as pltpu
 from jax.sharding import Mesh, PartitionSpec as P
 
 EX_DEV = 8
@@ -22,31 +24,73 @@
     return lax.ppermute(array, ("y", "core"), flat)
 
 
+def thirds(array):
+    first = array.astype(jnp.bfloat16)
+    left = array - first.astype(jnp.float32)
+    second = left.astype(jnp.bfloat16)
+    third = (left - second.astype(jnp.float32)).astype(jnp.bfloat16)
+    return first, second, third
+
+
+def features_kernel(token_ref, label_ref, left_ref, right_ref, out_ref, found):
+    rank = left_ref.shape[1]
+    lanes = 2 * rank
+    tokens = token_ref[0]
+    members = lax.broadcasted_iota(jnp.int32, (EX_DEV, tokens.shape[0]), 0) == label_ref[...]
+    chosen = members.astype(jnp.float32)
+    counts = jnp.sum(chosen, axis=1, keepdims=True)
+    chosen = chosen.astype(jnp.bfloat16)
+    outputs = tokens.T[rank:]
+    masked = jnp.concatenate([outputs * chosen[e : e + 1] for e in range(EX_DEV)], axis=0)
+    summed = jnp.dot(masked, tokens, preferred_element_type=jnp.float32)
+    gradient = jnp.concatenate(
+        [summed[e * rank : (e + 1) * rank] / counts[e : e + 1] for e in range(EX_DEV)], axis=0
+    )
+
+    right = right_ref[0].astype(jnp.float32)
+    right = jnp.concatenate([right, right], axis=1)
+    right = jnp.concatenate([right, jnp.zeros_like(right)], axis=0).astype(jnp.bfloat16)
+    turned = sum(
+        jnp.dot(part, right, preferred_element_type=jnp.float32) for part in thirds(gradient)
+    )
+
+    group = 256
+    left = left_ref[0].astype(jnp.float32)
+    left = jnp.concatenate([left] * (group // rank), axis=1)
+    left = jnp.concatenate([left] * (group // rank), axis=0)
+    row = lax.broadcasted_iota(jnp.int32, (group, group), 0) // rank
+    column = lax.broadcasted_iota(jnp.int32, (group, group), 1) // rank
+    left = jnp.where(row == column, left, 0.0).astype(jnp.bfloat16)
+    for start in range(0, EX_DEV * rank, group):
+        parts = jnp.concatenate(thirds(turned[start : start + group]), axis=1)
+        product = jnp.dot(left, parts, preferred_element_type=jnp.float32)
+        found[start : start + group, :] = (
+            product[:, :lanes] + product[:, lanes : 2 * lanes] + product[:, 2 * lanes :]
+        )
+
+    lane = lax.broadcasted_iota(jnp.int32, (EX_DEV, lanes), 1)
+    for pair in range(rank // 2):
+        even = found[pl.ds(2 * pair, EX_DEV, stride=rank), :]
+        odd = found[pl.ds(2 * pair + 1, EX_DEV, stride=rank), :]
+        tile = jnp.where(lane < rank, even, odd).astype(jnp.bfloat16)
+        for copy in range(out_ref.shape[0]):
+            out_ref[copy, :, pair * lanes : (pair + 1) * lanes] = tile
+
+
 def block_features(token_factors, example_ids, left_factor, right_factor):
-    proj_rank = left_factor.shape[1]
-    tokens_here = token_factors.shape[1]
-    examples = EX_DEV
-    labels = example_ids[0]
-    onehot = labels[:, None] == jnp.arange(examples, dtype=jnp.int32)[None, :]
-    selector = onehot.astype(jnp.bfloat16)
-    counts = jnp.sum(onehot.astype(jnp.float32), axis=0)
-    inputs = token_factors[0, :, :proj_rank]
-    outputs = token_factors[0, :, proj_rank:]
-    masked = (selector[:, :, None] * inputs[:, None, :]).reshape(tokens_here, examples * proj_rank)
-    summed = lax.dot_general(
-        outputs, masked, (((0,), (0,)), ((), ())), preferred_element_type=jnp.float32
-    )
-    gradient = (
-        summed.reshape(proj_rank, examples, proj_rank).transpose(1, 0, 2) / counts[:, None, None]
-    )
-    precond = jnp.einsum(
-        "ac,ecd,db->eab",
-        left_factor[0].astype(jnp.float32),
-        gradient,
-        right_factor[0].astype(jnp.float32),
-        precision=lax.Precision.HIGHEST,
-    )
-    return precond.reshape(examples, proj_rank * proj_rank).astype(jnp.bfloat16)
+    rank = left_factor.shape[1]
+    tokens = token_factors.shape[1]
+    return pl.pallas_call(
+        features_kernel,
+        out_shape=jax.ShapeDtypeStruct((Z_HI, EX_DEV, rank * rank), jnp.bfloat16),
+        scratch_shapes=[pltpu.VMEM((EX_DEV * rank, 2 * rank), jnp.float32)],
+        cost_estimate=pl.CostEstimate(
+            flops=2 * tokens * EX_DEV * rank * 2 * rank,
+            bytes_accessed=tokens * rank * 4 + Z_HI * EX_DEV * rank * rank * 2,
+            transcendentals=0,
+        ),
+        name="block_features",
+    )(token_factors, example_ids, left_factor, right_factor)
 
 
 def both_cores(mine, partner, core):
@@ -72,11 +116,6 @@
     )
 
 
-def to_all(array, axis):
-    copies = jnp.broadcast_to(array[None], (lax.axis_size(axis),) + array.shape)
-    return lax.all_to_all(copies, axis, 0, 0, tiled=False)
-
-
 def scored(queries, pieces):
     return lax.dot_general(
         queries, pieces, (((1,), (1,)), ((), ())), preferred_element_type=jnp.float32
@@ -89,7 +128,7 @@
     features = block_features(token_factors, example_ids, left_factor, right_factor)
     features, query_features = lax.optimization_barrier((features, query_features))
 
-    mine = to_all(features, "zh").reshape(Z_HI * EX_DEV, width)
+    mine = lax.all_to_all(features, "zh", 0, 0, tiled=False).reshape(Z_HI * EX_DEV, width)
     other = from_behind(query_features, "core", 1)
     queries = both_cores(query_features, other, core)
     place = placing(CORE * Y * Z_HI * EX_DEV, y)

time: 91.7 us -> 88.8 us (0.968)
  Pallas kernels: 0 us -> 3.6 us
  local copies, waits for them, and re-layouts: 3.06 us -> 0.12 us
  other arithmetic: 3.54 us -> 1.66 us
  matrix products: 7.09 us -> 5.61 us
    pallas_call x0 -> x1, Pallas kernels: none -> 3.6 us  [block_features(): pl.pallas_call(features_kernel, out_shape=jax.ShapeDtypeStruct((Z_HI, EX_...]
    dot_general x3 -> x0, matrix products: 1.49 us -> none  [the longest x1 0.94 us: block_features(): lax.dot_general(outputs, masked, (((0,), (0,)), ((), ())), preferred_elem...]
    mul x2 -> x0, local copies, waits for them, and re-layouts: 1.27 us -> none  [block_features(): selector[:, :, None] * inputs[:, None, :]]
where the time goes in v4:
time: 88.8 us; the launch traced here: 88.3 us
  starting transfers between devices  50.2 us (57%)
  blocking collectives  17 us (19%)
  waiting for transfers between devices  9.92 us (11%)
  matrix products  5.61 us (6%)
  Pallas kernels  3.6 us (4%)
  other arithmetic  1.66 us (2%)
    ppermute x7, starting transfers between devices, onward(): return lax.ppermute(array, ('y', 'core'), flat)  26.4 us
    all_to_all x1, blocking collectives, shards(): lax.all_to_all(parts, ('core',) + MP, 0, 0, tiled=False)  17 us
    all_to_all x1, starting transfers between devices, shards(): lax.all_to_all(features, 'zh', 0, 0, tiled=False)  15 us
    ppermute x2, starting transfers between devices, from_behind(): lax.ppermute(array, axis, [(i, (i + by) % length) for i in range(length)])  8.67 us
    all_to_all x1, waiting for transfers between devices, shards(): lax.all_to_all(features, 'zh', 0, 0, tiled=False)  6.46 us
    dot_general x8, matrix products, scored(): lax.dot_general(queries, pieces, (((1,), (1,)), ((), ())), preferred_elem...  4.64 us
    pallas_call x1, Pallas kernels, block_features(): pl.pallas_call(features_kernel, out_shape=jax.ShapeDtypeStruct((Z_HI, EX_...  3.6 us
    ppermute x7, waiting for transfers between devices, onward(): return lax.ppermute(array, ('y', 'core'), flat)  3.25 us
  transfers between devices with their start and end apart: 10, of which 3 were waited for; matrix products, arithmetic and copies ran while one was open for 6% of the time, Pallas kernels for 0%

profile of v4, /device:TPU:1, one launch (start us, length us, event | category | flops | bytes accessed | tf_op | source)
XLA Modules:
  0.0 88.3 jit_solution(488610934132936729)
XLA Ops:
  0.0 3.6 %block_features.1 = bf16[4,8,4096]{2,1,0:T(8,128)(2,1)} custom-call(bf16[1,2048,128]{2,1,0:T(8,128)(2,1)} %token_ref.1, s32[1,2048]{1,0:T(1,128)} %label_ref.1, bf16[1,64,64]{2,1,0:T(8,128)(2,1)} %left_ref.1, bf16[1,64,64]{2,1,0:T(8,128)(2,1)} %right_ref.1), custom_call_target="tpu_custom_call" | custom-call | flops 268435456 | bytes 786432 | tf_op jit(solution)/shard_map/block_features/pallas_call | solution.py:83
  3.6 15.0 %all-to-all-start = ((bf16[4,8,4096]{2,1,0:T(8,128)(2,1)}), bf16[4,8,4096]{2,1,0:T(8,128)(2,1)S(1)}, u32[]{:S(2)}, u32[]{:S(2)}) async-start(bf16[4,8,4096]{2,1,0:T(8,128)(2,1)} %block_features.1), calls=%async_computation | async-start | bytes 524288 | tf_op jit(solution)/shard_map/all_to_all | solution.py:131
  18.6 2.9 %collective-permute-start = (bf16[96,4096]{1,0:T(8,128)(2,1)}, bf16[96,4096]{1,0:T(8,128)(2,1)S(1)}, u32[]{:S(2)}, u32[]{:S(2)}) collective-permute-start(bf16[96,4096]{1,0:T(8,128)(2,1)} %param.9), channel_id=1, source_target_pairs={{0,12},{12,0},{1,13},{13,1},{2,14},{14,2},{3,15},{15,3},{4,16},{16... | collective-permute-start | bytes 2359304 | tf_op jit(solution)/shard_map/ppermute | solution.py:16
  21.6 1.3 %fusion.27 = bf16[512,512]{1,0:T(8,128)(2,1)S(1)} fusion(s32[512]{0:T(512)S(1)} %get-tuple-element.16, s32[512]{0:T(512)S(1)} %get-tuple-element.17, s32[512]{0:T(512)S(1)} %get-tuple-element.13, s32[512]{0:T(512)S(1)} %get-tuple-element.18, s32[512]{0:T(512)S(1)} %get-tuple-element.14, s32[512]{0:T(512)S(1)} %get-tuple-element.23, s32[]{:T(128)S(6)} %axis_index.28, ...), kind=kLoop, calls=%fused_computation.62 | loop fusion | flops 21233664 | bytes 542724 | tf_op jit(solution)/shard_map/convert_element_type | solution.py:114
  22.9 6.5 %all-to-all-done = bf16[4,8,4096]{2,1,0:T(8,128)(2,1)S(1)} async-done(((bf16[4,8,4096]{2,1,0:T(8,128)(2,1)}), bf16[4,8,4096]{2,1,0:T(8,128)(2,1)S(1)}, u32[]{:S(2)}, u32[]{:S(2)}) %all-to-all-start) | async-done | bytes 262176 | tf_op jit(solution)/shard_map/all_to_all | solution.py:131
  29.4 5.1 %collective-permute-start.1 = (bf16[32,4096]{1,0:T(8,128)(2,1)S(1)}, bf16[32,4096]{1,0:T(8,128)(2,1)S(1)}, u32[]{:S(2)}, u32[]{:S(2)}) collective-permute-start(bf16[32,4096]{1,0:T(8,128)(2,1)S(1)} %bitcast.28), channel_id=1, source_target_pairs={{0,24},{12,180},{24,48},{36,12},{48,72},{60,36},{72,96},{84,60},{9... | collective-permute-start | bytes 786440 | tf_op jit(solution)/shard_map/ppermute | solution.py:24
  34.5 5.8 %collective-permute-start.2 = (bf16[32,4096]{1,0:T(8,128)(2,1)S(1)}, bf16[32,4096]{1,0:T(8,128)(2,1)S(1)}, u32[]{:S(2)}, u32[]{:S(2)}) collective-permute-start(bf16[32,4096]{1,0:T(8,128)(2,1)S(1)} %bitcast.29), channel_id=1, source_target_pairs={{0,12},{12,0},{1,13},{13,1},{2,14},{14,2},{3,15},{15,3},{4,16},{16... | collective-permute-start | bytes 786440 | tf_op jit(solution)/shard_map/ppermute | solution.py:16
  40.6 0.6 fusion.9
  41.4 3.5 %collective-permute-start.3 = (bf16[32,4096]{1,0:T(8,128)(2,1)S(1)}, bf16[32,4096]{1,0:T(8,128)(2,1)S(1)}, u32[]{:S(2)}, u32[]{:S(2)}) collective-permute-start(bf16[32,4096]{1,0:T(8,128)(2,1)S(1)} %collective-permute-done.2), channel_id=1, source_target_pairs={{0,24},{12,180},{24,48},{36,12},{48,72},{60,36},{72,96},{84,60},{9... | collective-permute-start | bytes 786440 | tf_op jit(solution)/shard_map/ppermute | solution.py:24
  45.0 3.6 %collective-permute-start.4 = (bf16[32,4096]{1,0:T(8,128)(2,1)S(1)}, bf16[32,4096]{1,0:T(8,128)(2,1)S(1)}, u32[]{:S(2)}, u32[]{:S(2)}) collective-permute-start(bf16[32,4096]{1,0:T(8,128)(2,1)S(1)} %collective-permute-done.1), channel_id=1, source_target_pairs={{0,24},{12,180},{24,48},{36,12},{48,72},{60,36},{72,96},{84,60},{9... | collective-permute-start | bytes 786440 | tf_op jit(solution)/shard_map/ppermute | solution.py:24
  48.6 0.6 fusion.8
  49.2 4.0 %collective-permute-start.5 = (bf16[32,4096]{1,0:T(8,128)(2,1)S(1)}, bf16[32,4096]{1,0:T(8,128)(2,1)S(1)}, u32[]{:S(2)}, u32[]{:S(2)}) collective-permute-start(bf16[32,4096]{1,0:T(8,128)(2,1)S(1)} %collective-permute-done.3), channel_id=1, source_target_pairs={{0,24},{12,180},{24,48},{36,12},{48,72},{60,36},{72,96},{84,60},{9... | collective-permute-start | bytes 786440 | tf_op jit(solution)/shard_map/ppermute | solution.py:24
  53.3 0.6 fusion.7
  53.9 3.0 %collective-permute-start.6 = (bf16[32,4096]{1,0:T(8,128)(2,1)S(1)}, bf16[32,4096]{1,0:T(8,128)(2,1)S(1)}, u32[]{:S(2)}, u32[]{:S(2)}) collective-permute-start(bf16[32,4096]{1,0:T(8,128)(2,1)S(1)} %collective-permute-done.4), channel_id=1, source_target_pairs={{0,24},{12,180},{24,48},{36,12},{48,72},{60,36},{72,96},{84,60},{9... | collective-permute-start | bytes 786440 | tf_op jit(solution)/shard_map/ppermute | solution.py:24
  56.9 0.6 fusion.6
  57.5 4.0 %collective-permute-start.7 = (bf16[32,4096]{1,0:T(8,128)(2,1)S(1)}, bf16[32,4096]{1,0:T(8,128)(2,1)S(1)}, u32[]{:S(2)}, u32[]{:S(2)}) collective-permute-start(bf16[32,4096]{1,0:T(8,128)(2,1)S(1)} %collective-permute-done.5), channel_id=1, source_target_pairs={{0,24},{12,180},{24,48},{36,12},{48,72},{60,36},{72,96},{84,60},{9... | collective-permute-start | bytes 786440 | tf_op jit(solution)/shard_map/ppermute | solution.py:24
  61.6 0.6 fusion.5
  62.2 3.0 %collective-permute-start.8 = (bf16[32,4096]{1,0:T(8,128)(2,1)S(1)}, bf16[32,4096]{1,0:T(8,128)(2,1)S(1)}, u32[]{:S(2)}, u32[]{:S(2)}) collective-permute-start(bf16[32,4096]{1,0:T(8,128)(2,1)S(1)} %collective-permute-done.6), channel_id=1, source_target_pairs={{0,24},{12,180},{24,48},{36,12},{48,72},{60,36},{72,96},{84,60},{9... | collective-permute-start | bytes 786440 | tf_op jit(solution)/shard_map/ppermute | solution.py:24
  65.3 0.6 fusion.4
  65.9 0.6 fusion.3
  66.4 3.2 %collective-permute-done.8 = bf16[32,4096]{1,0:T(8,128)(2,1)S(1)} collective-permute-done((bf16[32,4096]{1,0:T(8,128)(2,1)S(1)}, bf16[32,4096]{1,0:T(8,128)(2,1)S(1)}, u32[]{:S(2)}, u32[]{:S(2)}) %collective-permute-start.8) | collective-permute-done | bytes 262176 | tf_op jit(solution)/shard_map/ppermute | solution.py:24
  69.6 0.6 fusion.2
  70.3 17.0 %all_to_all.10 = bf16[24,8,256]{2,1,0:T(8,128)(2,1)S(1)} all-to-all(bf16[24,8,256]{2,1,0:T(8,128)(2,1)S(1)} %bitcast.31), channel_id=1, replica_groups=mesh['zh'=4,'y'=8,'core'=2,'zl'=3,'x'=4] {'core','zl','x'}, dimensions={0} | all-to-all | bytes 196608 | tf_op jit(solution)/shard_map/all_to_all | solution.py:150
  87.5 0.8 fusion.1
  (19 shorter events, 0.9 us)
Async XLA Ops:
  0.0 40.3 %copy-start = (bf16[96,4096]{1,0:T(8,128)(2,1)S(1)}, bf16[96,4096]{1,0:T(8,128)(2,1)}, u32[]{:S(2)}) copy-start(bf16[96,4096]{1,0:T(8,128)(2,1)} %param.9) | copy-start | bytes 2359300
  3.6 25.8 %all-to-all-start = ((bf16[4,8,4096]{2,1,0:T(8,128)(2,1)}), bf16[4,8,4096]{2,1,0:T(8,128)(2,1)S(1)}, u32[]{:S(2)}, u32[]{:S(2)}) async-start(bf16[4,8,4096]{2,1,0:T(8,128)(2,1)} %block_features.1), calls=%async_computation | async-start | bytes 524288 | tf_op jit(solution)/shard_map/all_to_all | solution.py:131
  18.6 21.6 %collective-permute-start = (bf16[96,4096]{1,0:T(8,128)(2,1)}, bf16[96,4096]{1,0:T(8,128)(2,1)S(1)}, u32[]{:S(2)}, u32[]{:S(2)}) collective-permute-start(bf16[96,4096]{1,0:T(8,128)(2,1)} %param.9), channel_id=1, source_target_pairs={{0,12},{12,0},{1,13},{13,1},{2,14},{14,2},{3,15},{15,3},{4,16},{16... | collective-permute-start | bytes 2359304 | tf_op jit(solution)/shard_map/ppermute | solution.py:16
  29.4 15.6 %collective-permute-start.1 = (bf16[32,4096]{1,0:T(8,128)(2,1)S(1)}, bf16[32,4096]{1,0:T(8,128)(2,1)S(1)}, u32[]{:S(2)}, u32[]{:S(2)}) collective-permute-start(bf16[32,4096]{1,0:T(8,128)(2,1)S(1)} %bitcast.28), channel_id=1, source_target_pairs={{0,24},{12,180},{24,48},{36,12},{48,72},{60,36},{72,96},{84,60},{9... | collective-permute-start | bytes 786440 | tf_op jit(solution)/shard_map/ppermute | solution.py:24
  34.5 7.0 %collective-permute-start.2 = (bf16[32,4096]{1,0:T(8,128)(2,1)S(1)}, bf16[32,4096]{1,0:T(8,128)(2,1)S(1)}, u32[]{:S(2)}, u32[]{:S(2)}) collective-permute-start(bf16[32,4096]{1,0:T(8,128)(2,1)S(1)} %bitcast.29), channel_id=1, source_target_pairs={{0,12},{12,0},{1,13},{13,1},{2,14},{14,2},{3,15},{15,3},{4,16},{16... | collective-permute-start | bytes 786440 | tf_op jit(solution)/shard_map/ppermute | solution.py:16
  41.4 7.8 %collective-permute-start.3 = (bf16[32,4096]{1,0:T(8,128)(2,1)S(1)}, bf16[32,4096]{1,0:T(8,128)(2,1)S(1)}, u32[]{:S(2)}, u32[]{:S(2)}) collective-permute-start(bf16[32,4096]{1,0:T(8,128)(2,1)S(1)} %collective-permute-done.2), channel_id=1, source_target_pairs={{0,24},{12,180},{24,48},{36,12},{48,72},{60,36},{72,96},{84,60},{9... | collective-permute-start | bytes 786440 | tf_op jit(solution)/shard_map/ppermute | solution.py:24
  45.0 8.9 %collective-permute-start.4 = (bf16[32,4096]{1,0:T(8,128)(2,1)S(1)}, bf16[32,4096]{1,0:T(8,128)(2,1)S(1)}, u32[]{:S(2)}, u32[]{:S(2)}) collective-permute-start(bf16[32,4096]{1,0:T(8,128)(2,1)S(1)} %collective-permute-done.1), channel_id=1, source_target_pairs={{0,24},{12,180},{24,48},{36,12},{48,72},{60,36},{72,96},{84,60},{9... | collective-permute-start | bytes 786440 | tf_op jit(solution)/shard_map/ppermute | solution.py:24
  49.2 8.3 %collective-permute-start.5 = (bf16[32,4096]{1,0:T(8,128)(2,1)S(1)}, bf16[32,4096]{1,0:T(8,128)(2,1)S(1)}, u32[]{:S(2)}, u32[]{:S(2)}) collective-permute-start(bf16[32,4096]{1,0:T(8,128)(2,1)S(1)} %collective-permute-done.3), channel_id=1, source_target_pairs={{0,24},{12,180},{24,48},{36,12},{48,72},{60,36},{72,96},{84,60},{9... | collective-permute-start | bytes 786440 | tf_op jit(solution)/shard_map/ppermute | solution.py:24
  53.9 8.3 %collective-permute-start.6 = (bf16[32,4096]{1,0:T(8,128)(2,1)S(1)}, bf16[32,4096]{1,0:T(8,128)(2,1)S(1)}, u32[]{:S(2)}, u32[]{:S(2)}) collective-permute-start(bf16[32,4096]{1,0:T(8,128)(2,1)S(1)} %collective-permute-done.4), channel_id=1, source_target_pairs={{0,24},{12,180},{24,48},{36,12},{48,72},{60,36},{72,96},{84,60},{9... | collective-permute-start | bytes 786440 | tf_op jit(solution)/shard_map/ppermute | solution.py:24
  57.5 8.3 %collective-permute-start.7 = (bf16[32,4096]{1,0:T(8,128)(2,1)S(1)}, bf16[32,4096]{1,0:T(8,128)(2,1)S(1)}, u32[]{:S(2)}, u32[]{:S(2)}) collective-permute-start(bf16[32,4096]{1,0:T(8,128)(2,1)S(1)} %collective-permute-done.5), channel_id=1, source_target_pairs={{0,24},{12,180},{24,48},{36,12},{48,72},{60,36},{72,96},{84,60},{9... | collective-permute-start | bytes 786440 | tf_op jit(solution)/shard_map/ppermute | solution.py:24
  62.2 7.4 %collective-permute-start.8 = (bf16[32,4096]{1,0:T(8,128)(2,1)S(1)}, bf16[32,4096]{1,0:T(8,128)(2,1)S(1)}, u32[]{:S(2)}, u32[]{:S(2)}) collective-permute-start(bf16[32,4096]{1,0:T(8,128)(2,1)S(1)} %collective-permute-done.6), channel_id=1, source_target_pairs={{0,24},{12,180},{24,48},{36,12},{48,72},{60,36},{72,96},{84,60},{9... | collective-permute-start | bytes 786440 | tf_op jit(solution)/shard_map/ppermute | solution.py:24

commit v5 on v4

--- a/solution.py
+++ b/solution.py
@@ -16,12 +16,13 @@
     return lax.ppermute(array, axis, [(i, (i + by) % length) for i in range(length)])
 
 
-def onward(array):
-    steps = [
-        ((i, core), ((i + (1 if core == 0 else Y - 1)) % Y, core)) for i in range(Y) for core in range(CORE)
-    ]
-    flat = [(a[0] * CORE + a[1], b[0] * CORE + b[1]) for a, b in steps]
-    return lax.ppermute(array, ("y", "core"), flat)
+def onward(array, chips=1, swap=False):
+    pairs = []
+    for i in range(Y):
+        for core in range(CORE):
+            to = 1 - core if swap else core
+            pairs.append((i * CORE + core, (i + (chips if to == 0 else -chips)) % Y * CORE + to))
+    return lax.ppermute(array, ("y", "core"), pairs)
 
 
 def thirds(array):
@@ -134,14 +135,13 @@
     place = placing(CORE * Y * Z_HI * EX_DEV, y)
     mine, place = lax.optimization_barrier((mine, place))
 
-    partner = from_behind(mine, "core", 1)
-    pieces = [mine]
-    for step in range(1, Y // 2 + 1):
-        mine = onward(mine)
-        pieces.append(mine)
-        if step < Y // 2:
-            partner = onward(partner)
-            pieces.append(partner)
+    near, cross = onward(mine), onward(mine, swap=True)
+    pieces = [mine, near, cross]
+    near, cross = onward(near), onward(cross)
+    pieces += [near, cross]
+    far = onward(near, chips=2)
+    near, cross = onward(near), onward(cross)
+    pieces += [near, cross, far]
 
     scores = [scored(queries, piece) for piece in pieces]
     members = Z_LO * X

time: 88.8 us -> 88.4 us (level)
  starting transfers between devices: 50.2 us -> 47.1 us
  waiting for transfers between devices: 9.92 us -> 11.6 us
  blocking collectives: 17 us -> 18.1 us
    ppermute x2 -> x1, starting transfers between devices: 8.67 us -> 2.85 us  [from_behind(): lax.ppermute(array, axis, [(i, (i + by) % length) for i in range(length)])]
    ppermute x7, starting transfers between devices: 26.4 us -> 29.2 us  [onward(): return lax.ppermute(array, ('y', 'core'), pairs)]
    ppermute x7, waiting for transfers between devices: 3.25 us -> 5.13 us  [onward(): return lax.ppermute(array, ('y', 'core'), pairs)]
    all_to_all x1, blocking collectives: 17 us -> 18.1 us  [shards(): lax.all_to_all(parts, ('core',) + MP, 0, 0, tiled=False)]
  transfers between devices with their start and end apart: 10 -> 9, of which waited for: 3 -> 3; matrix products, arithmetic and copies ran while one was open for 6% -> 7% of each run, Pallas kernels for 0% -> 0%
where the time goes in v5:
time: 88.4 us; the launch traced here: 87.9 us
  starting transfers between devices  47.1 us (53%)
  blocking collectives  18.1 us (20%)
  waiting for transfers between devices  11.6 us (13%)
  matrix products  5.61 us (6%)
  Pallas kernels  3.6 us (4%)
  other arithmetic  1.66 us (2%)
    ppermute x7, starting transfers between devices, onward(): return lax.ppermute(array, ('y', 'core'), pairs)  29.2 us
    all_to_all x1, blocking collectives, shards(): lax.all_to_all(parts, ('core',) + MP, 0, 0, tiled=False)  18.1 us
    all_to_all x1, starting transfers between devices, shards(): lax.all_to_all(features, 'zh', 0, 0, tiled=False)  15 us
    all_to_all x1, waiting for transfers between devices, shards(): lax.all_to_all(features, 'zh', 0, 0, tiled=False)  6.46 us
    ppermute x7, waiting for transfers between devices, onward(): return lax.ppermute(array, ('y', 'core'), pairs)  5.13 us
    dot_general x8, matrix products, scored(): lax.dot_general(queries, pieces, (((1,), (1,)), ((), ())), preferred_elem...  4.64 us
    pallas_call x1, Pallas kernels, block_features(): pl.pallas_call(features_kernel, out_shape=jax.ShapeDtypeStruct((Z_HI, EX_...  3.6 us
    ppermute x1, starting transfers between devices, from_behind(): lax.ppermute(array, axis, [(i, (i + by) % length) for i in range(length)])  2.85 us
  transfers between devices with their start and end apart: 9, of which 3 were waited for; matrix products, arithmetic and copies ran while one was open for 7% of the time, Pallas kernels for 0%

profile of v5, /device:TPU:1, one launch (start us, length us, event | category | flops | bytes accessed | tf_op | source)
XLA Modules:
  0.0 87.9 jit_solution(7210157799364421257)
XLA Ops:
  0.0 3.6 %block_features.1 = bf16[4,8,4096]{2,1,0:T(8,128)(2,1)} custom-call(bf16[1,2048,128]{2,1,0:T(8,128)(2,1)} %token_ref.1, s32[1,2048]{1,0:T(1,128)} %label_ref.1, bf16[1,64,64]{2,1,0:T(8,128)(2,1)} %left_ref.1, bf16[1,64,64]{2,1,0:T(8,128)(2,1)} %right_ref.1), custom_call_target="tpu_custom_call" | custom-call | flops 268435456 | bytes 786432 | tf_op jit(solution)/shard_map/block_features/pallas_call | solution.py:84
  3.6 15.0 %all-to-all-start = ((bf16[4,8,4096]{2,1,0:T(8,128)(2,1)}), bf16[4,8,4096]{2,1,0:T(8,128)(2,1)S(1)}, u32[]{:S(2)}, u32[]{:S(2)}) async-start(bf16[4,8,4096]{2,1,0:T(8,128)(2,1)} %block_features.1), calls=%async_computation | async-start | bytes 524288 | tf_op jit(solution)/shard_map/all_to_all | solution.py:132
  18.7 2.9 %collective-permute-start = (bf16[96,4096]{1,0:T(8,128)(2,1)}, bf16[96,4096]{1,0:T(8,128)(2,1)S(1)}, u32[]{:S(2)}, u32[]{:S(2)}) collective-permute-start(bf16[96,4096]{1,0:T(8,128)(2,1)} %param.9), channel_id=1, source_target_pairs={{0,12},{12,0},{1,13},{13,1},{2,14},{14,2},{3,15},{15,3},{4,16},{16... | collective-permute-start | bytes 2359304 | tf_op jit(solution)/shard_map/ppermute | solution.py:16
  21.6 1.3 %fusion.27 = bf16[512,512]{1,0:T(8,128)(2,1)S(1)} fusion(s32[512]{0:T(512)S(1)} %get-tuple-element.16, s32[512]{0:T(512)S(1)} %get-tuple-element.17, s32[512]{0:T(512)S(1)} %get-tuple-element.13, s32[512]{0:T(512)S(1)} %get-tuple-element.18, s32[512]{0:T(512)S(1)} %get-tuple-element.14, s32[512]{0:T(512)S(1)} %get-tuple-element.23, s32[]{:T(128)S(6)} %axis_index.28, ...), kind=kLoop, calls=%fused_computation.62 | loop fusion | flops 21233664 | bytes 542724 | tf_op jit(solution)/shard_map/convert_element_type | solution.py:115
  22.9 6.5 %all-to-all-done = bf16[4,8,4096]{2,1,0:T(8,128)(2,1)S(1)} async-done(((bf16[4,8,4096]{2,1,0:T(8,128)(2,1)}), bf16[4,8,4096]{2,1,0:T(8,128)(2,1)S(1)}, u32[]{:S(2)}, u32[]{:S(2)}) %all-to-all-start) | async-done | bytes 262176 | tf_op jit(solution)/shard_map/all_to_all | solution.py:132
  29.4 5.1 %collective-permute-start.1 = (bf16[32,4096]{1,0:T(8,128)(2,1)S(1)}, bf16[32,4096]{1,0:T(8,128)(2,1)S(1)}, u32[]{:S(2)}, u32[]{:S(2)}) collective-permute-start(bf16[32,4096]{1,0:T(8,128)(2,1)S(1)} %bitcast.28), channel_id=1, source_target_pairs={{0,24},{12,180},{24,48},{36,12},{48,72},{60,36},{72,96},{84,60},{9... | collective-permute-start | bytes 786440 | tf_op jit(solution)/shard_map/ppermute | solution.py:25
  34.5 7.0 %collective-permute-start.2 = (bf16[32,4096]{1,0:T(8,128)(2,1)S(1)}, bf16[32,4096]{1,0:T(8,128)(2,1)S(1)}, u32[]{:S(2)}, u32[]{:S(2)}) collective-permute-start(bf16[32,4096]{1,0:T(8,128)(2,1)S(1)} %bitcast.29), channel_id=1, source_target_pairs={{0,180},{12,24},{24,12},{36,48},{48,36},{60,72},{72,60},{84,96},{9... | collective-permute-start | bytes 786440 | tf_op jit(solution)/shard_map/ppermute | solution.py:25
  41.5 0.3 maximum_select_fusion
  41.8 0.6 fusion.9
  42.4 3.3 %collective-permute-start.3 = (bf16[32,4096]{1,0:T(8,128)(2,1)S(1)}, bf16[32,4096]{1,0:T(8,128)(2,1)S(1)}, u32[]{:S(2)}, u32[]{:S(2)}) collective-permute-start(bf16[32,4096]{1,0:T(8,128)(2,1)S(1)} %collective-permute-done.1), channel_id=1, source_target_pairs={{0,24},{12,180},{24,48},{36,12},{48,72},{60,36},{72,96},{84,60},{9... | collective-permute-start | bytes 786440 | tf_op jit(solution)/shard_map/ppermute | solution.py:25
  45.7 0.6 fusion.8
  46.3 2.5 %collective-permute-start.4 = (bf16[32,4096]{1,0:T(8,128)(2,1)S(1)}, bf16[32,4096]{1,0:T(8,128)(2,1)S(1)}, u32[]{:S(2)}, u32[]{:S(2)}) collective-permute-start(bf16[32,4096]{1,0:T(8,128)(2,1)S(1)} %collective-permute-done.2), channel_id=1, source_target_pairs={{0,24},{12,180},{24,48},{36,12},{48,72},{60,36},{72,96},{84,60},{9... | collective-permute-start | bytes 786440 | tf_op jit(solution)/shard_map/ppermute | solution.py:25
  48.8 0.6 fusion.7
  49.5 4.5 %collective-permute-start.5 = (bf16[32,4096]{1,0:T(8,128)(2,1)S(1)}, bf16[32,4096]{1,0:T(8,128)(2,1)S(1)}, u32[]{:S(2)}, u32[]{:S(2)}) collective-permute-start(bf16[32,4096]{1,0:T(8,128)(2,1)S(1)} %collective-permute-done.3), channel_id=1, source_target_pairs={{0,24},{12,180},{24,48},{36,12},{48,72},{60,36},{72,96},{84,60},{9... | collective-permute-start | bytes 786440 | tf_op jit(solution)/shard_map/ppermute | solution.py:25
  54.0 3.9 %collective-permute-start.7 = (bf16[32,4096]{1,0:T(8,128)(2,1)S(1)}, bf16[32,4096]{1,0:T(8,128)(2,1)S(1)}, u32[]{:S(2)}, u32[]{:S(2)}) collective-permute-start(bf16[32,4096]{1,0:T(8,128)(2,1)S(1)} %collective-permute-done.3), channel_id=1, source_target_pairs={{0,48},{12,156},{24,72},{36,180},{48,96},{60,12},{72,120},{84,36},... | collective-permute-start | bytes 786440 | tf_op jit(solution)/shard_map/ppermute | solution.py:25
  57.9 0.6 fusion.6
  58.5 3.0 %collective-permute-start.6 = (bf16[32,4096]{1,0:T(8,128)(2,1)S(1)}, bf16[32,4096]{1,0:T(8,128)(2,1)S(1)}, u32[]{:S(2)}, u32[]{:S(2)}) collective-permute-start(bf16[32,4096]{1,0:T(8,128)(2,1)S(1)} %collective-permute-done.4), channel_id=1, source_target_pairs={{0,24},{12,180},{24,48},{36,12},{48,72},{60,36},{72,96},{84,60},{9... | collective-permute-start | bytes 786440 | tf_op jit(solution)/shard_map/ppermute | solution.py:25
  61.5 0.6 fusion.5
  62.1 0.6 fusion.4
  62.7 4.9 %collective-permute-done.6 = bf16[32,4096]{1,0:T(8,128)(2,1)S(1)} collective-permute-done((bf16[32,4096]{1,0:T(8,128)(2,1)S(1)}, bf16[32,4096]{1,0:T(8,128)(2,1)S(1)}, u32[]{:S(2)}, u32[]{:S(2)}) %collective-permute-start.6) | collective-permute-done | bytes 262176 | tf_op jit(solution)/shard_map/ppermute | solution.py:25
  67.6 0.6 fusion.3
  68.2 0.6 fusion.2
  68.9 18.1 %all_to_all.10 = bf16[24,8,256]{2,1,0:T(8,128)(2,1)S(1)} all-to-all(bf16[24,8,256]{2,1,0:T(8,128)(2,1)S(1)} %bitcast.31), channel_id=1, replica_groups=mesh['zh'=4,'y'=8,'core'=2,'zl'=3,'x'=4] {'core','zl','x'}, dimensions={0} | all-to-all | bytes 196608 | tf_op jit(solution)/shard_map/all_to_all | solution.py:150
  87.1 0.8 fusion.1
  (17 shorter events, 0.6 us)
Async XLA Ops:
  0.0 41.5 %copy-start = (bf16[96,4096]{1,0:T(8,128)(2,1)S(1)}, bf16[96,4096]{1,0:T(8,128)(2,1)}, u32[]{:S(2)}) copy-start(bf16[96,4096]{1,0:T(8,128)(2,1)} %param.9) | copy-start | bytes 2359300
  3.6 25.8 %all-to-all-start = ((bf16[4,8,4096]{2,1,0:T(8,128)(2,1)}), bf16[4,8,4096]{2,1,0:T(8,128)(2,1)S(1)}, u32[]{:S(2)}, u32[]{:S(2)}) async-start(bf16[4,8,4096]{2,1,0:T(8,128)(2,1)} %block_features.1), calls=%async_computation | async-start | bytes 524288 | tf_op jit(solution)/shard_map/all_to_all | solution.py:132
  18.7 22.8 %collective-permute-start = (bf16[96,4096]{1,0:T(8,128)(2,1)}, bf16[96,4096]{1,0:T(8,128)(2,1)S(1)}, u32[]{:S(2)}, u32[]{:S(2)}) collective-permute-start(bf16[96,4096]{1,0:T(8,128)(2,1)} %param.9), channel_id=1, source_target_pairs={{0,12},{12,0},{1,13},{13,1},{2,14},{14,2},{3,15},{15,3},{4,16},{16... | collective-permute-start | bytes 2359304 | tf_op jit(solution)/shard_map/ppermute | solution.py:16
  29.4 13.0 %collective-permute-start.1 = (bf16[32,4096]{1,0:T(8,128)(2,1)S(1)}, bf16[32,4096]{1,0:T(8,128)(2,1)S(1)}, u32[]{:S(2)}, u32[]{:S(2)}) collective-permute-start(bf16[32,4096]{1,0:T(8,128)(2,1)S(1)} %bitcast.28), channel_id=1, source_target_pairs={{0,24},{12,180},{24,48},{36,12},{48,72},{60,36},{72,96},{84,60},{9... | collective-permute-start | bytes 786440 | tf_op jit(solution)/shard_map/ppermute | solution.py:25
  34.5 11.8 %collective-permute-start.2 = (bf16[32,4096]{1,0:T(8,128)(2,1)S(1)}, bf16[32,4096]{1,0:T(8,128)(2,1)S(1)}, u32[]{:S(2)}, u32[]{:S(2)}) collective-permute-start(bf16[32,4096]{1,0:T(8,128)(2,1)S(1)} %bitcast.29), channel_id=1, source_target_pairs={{0,180},{12,24},{24,12},{36,48},{48,36},{60,72},{72,60},{84,96},{9... | collective-permute-start | bytes 786440 | tf_op jit(solution)/shard_map/ppermute | solution.py:25
  42.4 7.1 %collective-permute-start.3 = (bf16[32,4096]{1,0:T(8,128)(2,1)S(1)}, bf16[32,4096]{1,0:T(8,128)(2,1)S(1)}, u32[]{:S(2)}, u32[]{:S(2)}) collective-permute-start(bf16[32,4096]{1,0:T(8,128)(2,1)S(1)} %collective-permute-done.1), channel_id=1, source_target_pairs={{0,24},{12,180},{24,48},{36,12},{48,72},{60,36},{72,96},{84,60},{9... | collective-permute-start | bytes 786440 | tf_op jit(solution)/shard_map/ppermute | solution.py:25
  46.3 12.2 %collective-permute-start.4 = (bf16[32,4096]{1,0:T(8,128)(2,1)S(1)}, bf16[32,4096]{1,0:T(8,128)(2,1)S(1)}, u32[]{:S(2)}, u32[]{:S(2)}) collective-permute-start(bf16[32,4096]{1,0:T(8,128)(2,1)S(1)} %collective-permute-done.2), channel_id=1, source_target_pairs={{0,24},{12,180},{24,48},{36,12},{48,72},{60,36},{72,96},{84,60},{9... | collective-permute-start | bytes 786440 | tf_op jit(solution)/shard_map/ppermute | solution.py:25
  49.5 12.5 %collective-permute-start.5 = (bf16[32,4096]{1,0:T(8,128)(2,1)S(1)}, bf16[32,4096]{1,0:T(8,128)(2,1)S(1)}, u32[]{:S(2)}, u32[]{:S(2)}) collective-permute-start(bf16[32,4096]{1,0:T(8,128)(2,1)S(1)} %collective-permute-done.3), channel_id=1, source_target_pairs={{0,24},{12,180},{24,48},{36,12},{48,72},{60,36},{72,96},{84,60},{9... | collective-permute-start | bytes 786440 | tf_op jit(solution)/shard_map/ppermute | solution.py:25
  54.0 14.1 %collective-permute-start.7 = (bf16[32,4096]{1,0:T(8,128)(2,1)S(1)}, bf16[32,4096]{1,0:T(8,128)(2,1)S(1)}, u32[]{:S(2)}, u32[]{:S(2)}) collective-permute-start(bf16[32,4096]{1,0:T(8,128)(2,1)S(1)} %collective-permute-done.3), channel_id=1, source_target_pairs={{0,48},{12,156},{24,72},{36,180},{48,96},{60,12},{72,120},{84,36},... | collective-permute-start | bytes 786440 | tf_op jit(solution)/shard_map/ppermute | solution.py:25
  58.5 9.1 %collective-permute-start.6 = (bf16[32,4096]{1,0:T(8,128)(2,1)S(1)}, bf16[32,4096]{1,0:T(8,128)(2,1)S(1)}, u32[]{:S(2)}, u32[]{:S(2)}) collective-permute-start(bf16[32,4096]{1,0:T(8,128)(2,1)S(1)} %collective-permute-done.4), channel_id=1, source_target_pairs={{0,24},{12,180},{24,48},{36,12},{48,72},{60,36},{72,96},{84,60},{9... | collective-permute-start | bytes 786440 | tf_op jit(solution)/shard_map/ppermute | solution.py:25

commit v6 on v5

--- a/solution.py
+++ b/solution.py
@@ -16,12 +16,12 @@
     return lax.ppermute(array, axis, [(i, (i + by) % length) for i in range(length)])
 
 
-def onward(array, chips=1, swap=False):
+def onward(array, swap=False):
     pairs = []
     for i in range(Y):
         for core in range(CORE):
             to = 1 - core if swap else core
-            pairs.append((i * CORE + core, (i + (chips if to == 0 else -chips)) % Y * CORE + to))
+            pairs.append((i * CORE + core, (i + (1 if to == 0 else Y - 1)) % Y * CORE + to))
     return lax.ppermute(array, ("y", "core"), pairs)
 
 
@@ -137,11 +137,10 @@
 
     near, cross = onward(mine), onward(mine, swap=True)
     pieces = [mine, near, cross]
-    near, cross = onward(near), onward(cross)
-    pieces += [near, cross]
-    far = onward(near, chips=2)
-    near, cross = onward(near), onward(cross)
-    pieces += [near, cross, far]
+    for _ in (2, 3):
+        near, cross = onward(near), onward(cross)
+        pieces += [near, cross]
+    pieces.append(onward(near))
 
     scores = [scored(queries, piece) for piece in pieces]
     members = Z_LO * X

time: 88.4 us -> 88.2 us (level)
  waiting for transfers between devices: 11.6 us -> 8.94 us
  blocking collectives: 18.1 us -> 20.5 us
    ppermute x7, waiting for transfers between devices: 5.13 us -> 2.48 us  [onward(): return lax.ppermute(array, ('y', 'core'), pairs)]
    all_to_all x1, blocking collectives: 18.1 us -> 20.5 us  [shards(): lax.all_to_all(parts, ('core',) + MP, 0, 0, tiled=False)]
  transfers between devices with their start and end apart: 9 -> 9, of which waited for: 3 -> 4; matrix products, arithmetic and copies ran while one was open for 7% -> 7% of each run, Pallas kernels for 0% -> 0%
where the time goes in v6:
time: 88.2 us; the launch traced here: 87.8 us
  starting transfers between devices  47.2 us (54%)
  blocking collectives  20.5 us (23%)
  waiting for transfers between devices  8.94 us (10%)
  matrix products  5.61 us (6%)
  Pallas kernels  3.6 us (4%)
  other arithmetic  1.66 us (2%)
    ppermute x7, starting transfers between devices, onward(): return lax.ppermute(array, ('y', 'core'), pairs)  29.3 us
    all_to_all x1, blocking collectives, shards(): lax.all_to_all(parts, ('core',) + MP, 0, 0, tiled=False)  20.5 us
    all_to_all x1, starting transfers between devices, shards(): lax.all_to_all(features, 'zh', 0, 0, tiled=False)  15 us
    all_to_all x1, waiting for transfers between devices, shards(): lax.all_to_all(features, 'zh', 0, 0, tiled=False)  6.46 us
    dot_general x8, matrix products, scored(): lax.dot_general(queries, pieces, (((1,), (1,)), ((), ())), preferred_elem...  4.64 us
    pallas_call x1, Pallas kernels, block_features(): pl.pallas_call(features_kernel, out_shape=jax.ShapeDtypeStruct((Z_HI, EX_...  3.6 us
    ppermute x1, starting transfers between devices, from_behind(): lax.ppermute(array, axis, [(i, (i + by) % length) for i in range(length)])  2.85 us
    ppermute x7, waiting for transfers between devices, onward(): return lax.ppermute(array, ('y', 'core'), pairs)  2.48 us
  transfers between devices with their start and end apart: 9, of which 4 were waited for; matrix products, arithmetic and copies ran while one was open for 7% of the time, Pallas kernels for 0%

profile of v6, /device:TPU:1, one launch (start us, length us, event | category | flops | bytes accessed | tf_op | source)
XLA Modules:
  0.0 87.8 jit_solution(9715554903045695053)
XLA Ops:
  0.0 3.6 %block_features.1 = bf16[4,8,4096]{2,1,0:T(8,128)(2,1)} custom-call(bf16[1,2048,128]{2,1,0:T(8,128)(2,1)} %token_ref.1, s32[1,2048]{1,0:T(1,128)} %label_ref.1, bf16[1,64,64]{2,1,0:T(8,128)(2,1)} %left_ref.1, bf16[1,64,64]{2,1,0:T(8,128)(2,1)} %right_ref.1), custom_call_target="tpu_custom_call" | custom-call | flops 268435456 | bytes 786432 | tf_op jit(solution)/shard_map/block_features/pallas_call | solution.py:84
  3.6 15.0 %all-to-all-start = ((bf16[4,8,4096]{2,1,0:T(8,128)(2,1)}), bf16[4,8,4096]{2,1,0:T(8,128)(2,1)S(1)}, u32[]{:S(2)}, u32[]{:S(2)}) async-start(bf16[4,8,4096]{2,1,0:T(8,128)(2,1)} %block_features.1), calls=%async_computation | async-start | bytes 524288 | tf_op jit(solution)/shard_map/all_to_all | solution.py:132
  18.7 2.9 %collective-permute-start = (bf16[96,4096]{1,0:T(8,128)(2,1)}, bf16[96,4096]{1,0:T(8,128)(2,1)S(1)}, u32[]{:S(2)}, u32[]{:S(2)}) collective-permute-start(bf16[96,4096]{1,0:T(8,128)(2,1)} %param.9), channel_id=1, source_target_pairs={{0,12},{12,0},{1,13},{13,1},{2,14},{14,2},{3,15},{15,3},{4,16},{16... | collective-permute-start | bytes 2359304 | tf_op jit(solution)/shard_map/ppermute | solution.py:16
  21.6 1.3 %fusion.27 = bf16[512,512]{1,0:T(8,128)(2,1)S(1)} fusion(s32[512]{0:T(512)S(1)} %get-tuple-element.16, s32[512]{0:T(512)S(1)} %get-tuple-element.17, s32[512]{0:T(512)S(1)} %get-tuple-element.13, s32[512]{0:T(512)S(1)} %get-tuple-element.18, s32[512]{0:T(512)S(1)} %get-tuple-element.14, s32[512]{0:T(512)S(1)} %get-tuple-element.23, s32[]{:T(128)S(6)} %axis_index.28, ...), kind=kLoop, calls=%fused_computation.62 | loop fusion | flops 21233664 | bytes 542724 | tf_op jit(solution)/shard_map/convert_element_type | solution.py:115
  22.9 6.5 %all-to-all-done = bf16[4,8,4096]{2,1,0:T(8,128)(2,1)S(1)} async-done(((bf16[4,8,4096]{2,1,0:T(8,128)(2,1)}), bf16[4,8,4096]{2,1,0:T(8,128)(2,1)S(1)}, u32[]{:S(2)}, u32[]{:S(2)}) %all-to-all-start) | async-done | bytes 262176 | tf_op jit(solution)/shard_map/all_to_all | solution.py:132
  29.4 5.1 %collective-permute-start.1 = (bf16[32,4096]{1,0:T(8,128)(2,1)S(1)}, bf16[32,4096]{1,0:T(8,128)(2,1)S(1)}, u32[]{:S(2)}, u32[]{:S(2)}) collective-permute-start(bf16[32,4096]{1,0:T(8,128)(2,1)S(1)} %bitcast.28), channel_id=1, source_target_pairs={{0,24},{12,180},{24,48},{36,12},{48,72},{60,36},{72,96},{84,60},{9... | collective-permute-start | bytes 786440 | tf_op jit(solution)/shard_map/ppermute | solution.py:25
  34.5 7.0 %collective-permute-start.2 = (bf16[32,4096]{1,0:T(8,128)(2,1)S(1)}, bf16[32,4096]{1,0:T(8,128)(2,1)S(1)}, u32[]{:S(2)}, u32[]{:S(2)}) collective-permute-start(bf16[32,4096]{1,0:T(8,128)(2,1)S(1)} %bitcast.29), channel_id=1, source_target_pairs={{0,180},{12,24},{24,12},{36,48},{48,36},{60,72},{72,60},{84,96},{9... | collective-permute-start | bytes 786440 | tf_op jit(solution)/shard_map/ppermute | solution.py:25
  41.5 0.3 maximum_select_fusion
  41.8 0.6 fusion.9
  42.4 3.3 %collective-permute-start.3 = (bf16[32,4096]{1,0:T(8,128)(2,1)S(1)}, bf16[32,4096]{1,0:T(8,128)(2,1)S(1)}, u32[]{:S(2)}, u32[]{:S(2)}) collective-permute-start(bf16[32,4096]{1,0:T(8,128)(2,1)S(1)} %collective-permute-done.1), channel_id=1, source_target_pairs={{0,24},{12,180},{24,48},{36,12},{48,72},{60,36},{72,96},{84,60},{9... | collective-permute-start | bytes 786440 | tf_op jit(solution)/shard_map/ppermute | solution.py:25
  45.7 0.6 fusion.8
  46.3 2.5 %collective-permute-start.4 = (bf16[32,4096]{1,0:T(8,128)(2,1)S(1)}, bf16[32,4096]{1,0:T(8,128)(2,1)S(1)}, u32[]{:S(2)}, u32[]{:S(2)}) collective-permute-start(bf16[32,4096]{1,0:T(8,128)(2,1)S(1)} %collective-permute-done.2), channel_id=1, source_target_pairs={{0,24},{12,180},{24,48},{36,12},{48,72},{60,36},{72,96},{84,60},{9... | collective-permute-start | bytes 786440 | tf_op jit(solution)/shard_map/ppermute | solution.py:25
  48.8 0.6 fusion.7
  49.5 4.5 %collective-permute-start.5 = (bf16[32,4096]{1,0:T(8,128)(2,1)S(1)}, bf16[32,4096]{1,0:T(8,128)(2,1)S(1)}, u32[]{:S(2)}, u32[]{:S(2)}) collective-permute-start(bf16[32,4096]{1,0:T(8,128)(2,1)S(1)} %collective-permute-done.3), channel_id=1, source_target_pairs={{0,24},{12,180},{24,48},{36,12},{48,72},{60,36},{72,96},{84,60},{9... | collective-permute-start | bytes 786440 | tf_op jit(solution)/shard_map/ppermute | solution.py:25
  54.0 0.6 fusion.6
  54.6 2.5 %collective-permute-start.6 = (bf16[32,4096]{1,0:T(8,128)(2,1)S(1)}, bf16[32,4096]{1,0:T(8,128)(2,1)S(1)}, u32[]{:S(2)}, u32[]{:S(2)}) collective-permute-start(bf16[32,4096]{1,0:T(8,128)(2,1)S(1)} %collective-permute-done.4), channel_id=1, source_target_pairs={{0,24},{12,180},{24,48},{36,12},{48,72},{60,36},{72,96},{84,60},{9... | collective-permute-start | bytes 786440 | tf_op jit(solution)/shard_map/ppermute | solution.py:25
  57.1 0.6 fusion.5
  57.9 4.5 %collective-permute-start.7 = (bf16[32,4096]{1,0:T(8,128)(2,1)S(1)}, bf16[32,4096]{1,0:T(8,128)(2,1)S(1)}, u32[]{:S(2)}, u32[]{:S(2)}) collective-permute-start(bf16[32,4096]{1,0:T(8,128)(2,1)S(1)} %collective-permute-done.5), channel_id=1, source_target_pairs={{0,24},{12,180},{24,48},{36,12},{48,72},{60,36},{72,96},{84,60},{9... | collective-permute-start | bytes 786440 | tf_op jit(solution)/shard_map/ppermute | solution.py:25
  62.4 0.6 fusion.4
  63.0 0.6 fusion.3
  63.5 2.1 %collective-permute-done.7 = bf16[32,4096]{1,0:T(8,128)(2,1)S(1)} collective-permute-done((bf16[32,4096]{1,0:T(8,128)(2,1)S(1)}, bf16[32,4096]{1,0:T(8,128)(2,1)S(1)}, u32[]{:S(2)}, u32[]{:S(2)}) %collective-permute-start.7) | collective-permute-done | bytes 262176 | tf_op jit(solution)/shard_map/ppermute | solution.py:25
  65.7 0.6 fusion.2
  66.4 20.5 %all_to_all.10 = bf16[24,8,256]{2,1,0:T(8,128)(2,1)S(1)} all-to-all(bf16[24,8,256]{2,1,0:T(8,128)(2,1)S(1)} %bitcast.31), channel_id=1, replica_groups=mesh['zh'=4,'y'=8,'core'=2,'zl'=3,'x'=4] {'core','zl','x'}, dimensions={0} | all-to-all | bytes 196608 | tf_op jit(solution)/shard_map/all_to_all | solution.py:149
  87.0 0.8 fusion.1
  (17 shorter events, 0.7 us)
Async XLA Ops:
  0.0 41.5 %copy-start = (bf16[96,4096]{1,0:T(8,128)(2,1)S(1)}, bf16[96,4096]{1,0:T(8,128)(2,1)}, u32[]{:S(2)}) copy-start(bf16[96,4096]{1,0:T(8,128)(2,1)} %param.9) | copy-start | bytes 2359300
  3.6 25.8 %all-to-all-start = ((bf16[4,8,4096]{2,1,0:T(8,128)(2,1)}), bf16[4,8,4096]{2,1,0:T(8,128)(2,1)S(1)}, u32[]{:S(2)}, u32[]{:S(2)}) async-start(bf16[4,8,4096]{2,1,0:T(8,128)(2,1)} %block_features.1), calls=%async_computation | async-start | bytes 524288 | tf_op jit(solution)/shard_map/all_to_all | solution.py:132
  18.7 22.8 %collective-permute-start = (bf16[96,4096]{1,0:T(8,128)(2,1)}, bf16[96,4096]{1,0:T(8,128)(2,1)S(1)}, u32[]{:S(2)}, u32[]{:S(2)}) collective-permute-start(bf16[96,4096]{1,0:T(8,128)(2,1)} %param.9), channel_id=1, source_target_pairs={{0,12},{12,0},{1,13},{13,1},{2,14},{14,2},{3,15},{15,3},{4,16},{16... | collective-permute-start | bytes 2359304 | tf_op jit(solution)/shard_map/ppermute | solution.py:16
  29.4 13.0 %collective-permute-start.1 = (bf16[32,4096]{1,0:T(8,128)(2,1)S(1)}, bf16[32,4096]{1,0:T(8,128)(2,1)S(1)}, u32[]{:S(2)}, u32[]{:S(2)}) collective-permute-start(bf16[32,4096]{1,0:T(8,128)(2,1)S(1)} %bitcast.28), channel_id=1, source_target_pairs={{0,24},{12,180},{24,48},{36,12},{48,72},{60,36},{72,96},{84,60},{9... | collective-permute-start | bytes 786440 | tf_op jit(solution)/shard_map/ppermute | solution.py:25
  34.5 11.8 %collective-permute-start.2 = (bf16[32,4096]{1,0:T(8,128)(2,1)S(1)}, bf16[32,4096]{1,0:T(8,128)(2,1)S(1)}, u32[]{:S(2)}, u32[]{:S(2)}) collective-permute-start(bf16[32,4096]{1,0:T(8,128)(2,1)S(1)} %bitcast.29), channel_id=1, source_target_pairs={{0,180},{12,24},{24,12},{36,48},{48,36},{60,72},{72,60},{84,96},{9... | collective-permute-start | bytes 786440 | tf_op jit(solution)/shard_map/ppermute | solution.py:25
  42.4 7.1 %collective-permute-start.3 = (bf16[32,4096]{1,0:T(8,128)(2,1)S(1)}, bf16[32,4096]{1,0:T(8,128)(2,1)S(1)}, u32[]{:S(2)}, u32[]{:S(2)}) collective-permute-start(bf16[32,4096]{1,0:T(8,128)(2,1)S(1)} %collective-permute-done.1), channel_id=1, source_target_pairs={{0,24},{12,180},{24,48},{36,12},{48,72},{60,36},{72,96},{84,60},{9... | collective-permute-start | bytes 786440 | tf_op jit(solution)/shard_map/ppermute | solution.py:25
  46.3 8.3 %collective-permute-start.4 = (bf16[32,4096]{1,0:T(8,128)(2,1)S(1)}, bf16[32,4096]{1,0:T(8,128)(2,1)S(1)}, u32[]{:S(2)}, u32[]{:S(2)}) collective-permute-start(bf16[32,4096]{1,0:T(8,128)(2,1)S(1)} %collective-permute-done.2), channel_id=1, source_target_pairs={{0,24},{12,180},{24,48},{36,12},{48,72},{60,36},{72,96},{84,60},{9... | collective-permute-start | bytes 786440 | tf_op jit(solution)/shard_map/ppermute | solution.py:25
  49.5 8.3 %collective-permute-start.5 = (bf16[32,4096]{1,0:T(8,128)(2,1)S(1)}, bf16[32,4096]{1,0:T(8,128)(2,1)S(1)}, u32[]{:S(2)}, u32[]{:S(2)}) collective-permute-start(bf16[32,4096]{1,0:T(8,128)(2,1)S(1)} %collective-permute-done.3), channel_id=1, source_target_pairs={{0,24},{12,180},{24,48},{36,12},{48,72},{60,36},{72,96},{84,60},{9... | collective-permute-start | bytes 786440 | tf_op jit(solution)/shard_map/ppermute | solution.py:25
  54.6 8.3 %collective-permute-start.6 = (bf16[32,4096]{1,0:T(8,128)(2,1)S(1)}, bf16[32,4096]{1,0:T(8,128)(2,1)S(1)}, u32[]{:S(2)}, u32[]{:S(2)}) collective-permute-start(bf16[32,4096]{1,0:T(8,128)(2,1)S(1)} %collective-permute-done.4), channel_id=1, source_target_pairs={{0,24},{12,180},{24,48},{36,12},{48,72},{60,36},{72,96},{84,60},{9... | collective-permute-start | bytes 786440 | tf_op jit(solution)/shard_map/ppermute | solution.py:25
  57.9 7.8 %collective-permute-start.7 = (bf16[32,4096]{1,0:T(8,128)(2,1)S(1)}, bf16[32,4096]{1,0:T(8,128)(2,1)S(1)}, u32[]{:S(2)}, u32[]{:S(2)}) collective-permute-start(bf16[32,4096]{1,0:T(8,128)(2,1)S(1)} %collective-permute-done.5), channel_id=1, source_target_pairs={{0,24},{12,180},{24,48},{36,12},{48,72},{60,36},{72,96},{84,60},{9... | collective-permute-start | bytes 786440 | tf_op jit(solution)/shard_map/ppermute | solution.py:25

commit v7 on v6

--- a/solution.py
+++ b/solution.py
@@ -6,6 +6,7 @@
 from jax.sharding import Mesh, PartitionSpec as P
 
 EX_DEV = 8
+LOADS, STORES = 4, 2
 Z_HI, Y, CORE, Z_LO, X = 4, 8, 2, 3, 4
 DP = ("zh", "y", "core")
 MP = ("zl", "x")
@@ -33,27 +34,28 @@
     return first, second, third
 
 
-def features_kernel(token_ref, label_ref, left_ref, right_ref, out_ref, found):
+def features_kernel(
+    token_ref, label_ref, left_ref, right_ref, out_ref, held, found, made, load_sems, store_sems
+):
     rank = left_ref.shape[1]
     lanes = 2 * rank
-    tokens = token_ref[0]
-    members = lax.broadcasted_iota(jnp.int32, (EX_DEV, tokens.shape[0]), 0) == label_ref[...]
+    tokens = held.shape[0] // LOADS
+
+    def load(i):
+        rows = pl.ds(i * tokens, tokens)
+        return pltpu.make_async_copy(token_ref.at[0, rows, :], held.at[rows, :], load_sems.at[i])
+
+    for i in range(LOADS):
+        load(i).start()
+
+    members = lax.broadcasted_iota(jnp.int32, (EX_DEV, held.shape[0]), 0) == label_ref[...]
     chosen = members.astype(jnp.float32)
     counts = jnp.sum(chosen, axis=1, keepdims=True)
     chosen = chosen.astype(jnp.bfloat16)
-    outputs = tokens.T[rank:]
-    masked = jnp.concatenate([outputs * chosen[e : e + 1] for e in range(EX_DEV)], axis=0)
-    summed = jnp.dot(masked, tokens, preferred_element_type=jnp.float32)
-    gradient = jnp.concatenate(
-        [summed[e * rank : (e + 1) * rank] / counts[e : e + 1] for e in range(EX_DEV)], axis=0
-    )
 
     right = right_ref[0].astype(jnp.float32)
     right = jnp.concatenate([right, right], axis=1)
     right = jnp.concatenate([right, jnp.zeros_like(right)], axis=0).astype(jnp.bfloat16)
-    turned = sum(
-        jnp.dot(part, right, preferred_element_type=jnp.float32) for part in thirds(gradient)
-    )
 
     group = 256
     left = left_ref[0].astype(jnp.float32)
@@ -62,6 +64,22 @@
     row = lax.broadcasted_iota(jnp.int32, (group, group), 0) // rank
     column = lax.broadcasted_iota(jnp.int32, (group, group), 1) // rank
     left = jnp.where(row == column, left, 0.0).astype(jnp.bfloat16)
+
+    summed = None
+    for i in range(LOADS):
+        load(i).wait()
+        here = held[i * tokens : (i + 1) * tokens, :]
+        outputs = here.T[rank:]
+        picked = chosen[:, i * tokens : (i + 1) * tokens]
+        masked = jnp.concatenate([outputs * picked[e : e + 1] for e in range(EX_DEV)], axis=0)
+        product = jnp.dot(masked, here, preferred_element_type=jnp.float32)
+        summed = product if summed is None else summed + product
+    gradient = jnp.concatenate(
+        [summed[e * rank : (e + 1) * rank] / counts[e : e + 1] for e in range(EX_DEV)], axis=0
+    )
+    turned = sum(
+        jnp.dot(part, right, preferred_element_type=jnp.float32) for part in thirds(gradient)
+    )
     for start in range(0, EX_DEV * rank, group):
         parts = jnp.concatenate(thirds(turned[start : start + group]), axis=1)
         product = jnp.dot(left, parts, preferred_element_type=jnp.float32)
@@ -69,22 +87,43 @@
             product[:, :lanes] + product[:, lanes : 2 * lanes] + product[:, 2 * lanes :]
         )
 
+    def store(i, copy):
+        columns = pl.ds(i * (made.shape[1] // STORES), made.shape[1] // STORES)
+        return pltpu.make_async_copy(
+            made.at[:, columns], out_ref.at[copy, :, columns], store_sems.at[i, copy]
+        )
+
     lane = lax.broadcasted_iota(jnp.int32, (EX_DEV, lanes), 1)
-    for pair in range(rank // 2):
-        even = found[pl.ds(2 * pair, EX_DEV, stride=rank), :]
-        odd = found[pl.ds(2 * pair + 1, EX_DEV, stride=rank), :]
-        tile = jnp.where(lane < rank, even, odd).astype(jnp.bfloat16)
-        for copy in range(out_ref.shape[0]):
-            out_ref[copy, :, pair * lanes : (pair + 1) * lanes] = tile
+    pairs = rank // 2 // STORES
+    for i in range(STORES):
+        for pair in range(i * pairs, (i + 1) * pairs):
+            even = found[pl.ds(2 * pair, EX_DEV, stride=rank), :]
+            odd = found[pl.ds(2 * pair + 1, EX_DEV, stride=rank), :]
+            tile = jnp.where(lane < rank, even, odd).astype(jnp.bfloat16)
+            made[:, pair * lanes : (pair + 1) * lanes] = tile
+        for copy in range(Z_HI):
+            store(i, copy).start()
+    for i in range(STORES):
+        for copy in range(Z_HI):
+            store(i, copy).wait()
 
 
 def block_features(token_factors, example_ids, left_factor, right_factor):
     rank = left_factor.shape[1]
     tokens = token_factors.shape[1]
+    vmem = pl.BlockSpec(memory_space=pltpu.VMEM)
     return pl.pallas_call(
         features_kernel,
         out_shape=jax.ShapeDtypeStruct((Z_HI, EX_DEV, rank * rank), jnp.bfloat16),
-        scratch_shapes=[pltpu.VMEM((EX_DEV * rank, 2 * rank), jnp.float32)],
+        in_specs=[pl.BlockSpec(memory_space=pl.ANY), vmem, vmem, vmem],
+        out_specs=pl.BlockSpec(memory_space=pl.ANY),
+        scratch_shapes=[
+            pltpu.VMEM((tokens, 2 * rank), jnp.bfloat16),
+            pltpu.VMEM((EX_DEV * rank, 2 * rank), jnp.float32),
+            pltpu.VMEM((EX_DEV, rank * rank), jnp.bfloat16),
+            pltpu.SemaphoreType.DMA((LOADS,)),
+            pltpu.SemaphoreType.DMA((STORES, Z_HI)),
+        ],
         cost_estimate=pl.CostEstimate(
             flops=2 * tokens * EX_DEV * rank * 2 * rank,
             bytes_accessed=tokens * rank * 4 + Z_HI * EX_DEV * rank * rank * 2,
@@ -147,14 +186,11 @@
     parts = jnp.concatenate([part.astype(jnp.bfloat16) for part in scores], axis=1)
     parts = parts.reshape(CORE * members, rows // members, -1)
     traded = lax.all_to_all(parts, ("core",) + MP, 0, 0, tiled=False).reshape(CORE, rows, -1)
-    placed = sum(
-        lax.dot_general(
-            traded[i],
-            place[i * traded.shape[2] : (i + 1) * traded.shape[2]],
-            (((1,), (0,)), ((), ())),
-            preferred_element_type=jnp.float32,
-        )
-        for i in range(CORE)
+    placed = lax.dot_general(
+        jnp.concatenate([traded[i] for i in range(CORE)], axis=1),
+        place,
+        (((1,), (0,)), ((), ())),
+        preferred_element_type=jnp.float32,
     )
     return jnp.sum(placed.reshape(members, rows // members, -1), axis=0)
 

time: 88.2 us -> 89.3 us (1.012)
  Pallas kernels: 3.6 us -> 4.65 us
    pallas_call x1, Pallas kernels: 3.6 us -> 4.65 us  [block_features(): pl.pallas_call(features_kernel, out_shape=jax.ShapeDtypeStruct((Z_HI, EX_...]
  transfers between devices with their start and end apart: 9 -> 9, of which waited for: 4 -> 4; matrix products, arithmetic and copies ran while one was open for 7% -> 6% of each run, Pallas kernels for 0% -> 0%
where the time goes in v7:
time: 89.3 us; the launch traced here: 88.7 us
  starting transfers between devices  47.2 us (53%)
  blocking collectives  20.4 us (23%)
  waiting for transfers between devices  8.93 us (10%)
  matrix products  5.48 us (6%)
  Pallas kernels  4.65 us (5%)
  other arithmetic  1.66 us (2%)
    ppermute x7, starting transfers between devices, onward(): return lax.ppermute(array, ('y', 'core'), pairs)  29.3 us
    all_to_all x1, blocking collectives, shards(): lax.all_to_all(parts, ('core',) + MP, 0, 0, tiled=False)  20.4 us
    all_to_all x1, starting transfers between devices, shards(): lax.all_to_all(features, 'zh', 0, 0, tiled=False)  15.1 us
    all_to_all x1, waiting for transfers between devices, shards(): lax.all_to_all(features, 'zh', 0, 0, tiled=False)  6.46 us
    pallas_call x1, Pallas kernels, block_features(): pl.pallas_call(features_kernel, out_shape=jax.ShapeDtypeStruct((Z_HI, EX_...  4.65 us
    dot_general x8, matrix products, scored(): lax.dot_general(queries, pieces, (((1,), (1,)), ((), ())), preferred_elem...  4.65 us
    ppermute x1, starting transfers between devices, from_behind(): lax.ppermute(array, axis, [(i, (i + by) % length) for i in range(length)])  2.85 us
    ppermute x7, waiting for transfers between devices, onward(): return lax.ppermute(array, ('y', 'core'), pairs)  2.47 us
  transfers between devices with their start and end apart: 9, of which 4 were waited for; matrix products, arithmetic and copies ran while one was open for 6% of the time, Pallas kernels for 0%

profile of v7, /device:TPU:1, one launch (start us, length us, event | category | flops | bytes accessed | tf_op | source)
XLA Modules:
  0.0 88.7 jit_solution(11865611255653833533)
XLA Ops:
  0.0 4.6 %block_features.1 = bf16[4,8,4096]{2,1,0:T(8,128)(2,1)} custom-call(bf16[1,2048,128]{2,1,0:T(8,128)(2,1)} %token_ref.1, s32[1,2048]{1,0:T(1,128)} %label_ref.1, bf16[1,64,64]{2,1,0:T(8,128)(2,1)} %left_ref.1, bf16[1,64,64]{2,1,0:T(8,128)(2,1)} %right_ref.1), custom_call_target="tpu_custom_call" | custom-call | flops 268435456 | bytes 786432 | tf_op jit(solution)/shard_map/block_features/pallas_call | solution.py:115
  4.7 15.1 %all-to-all-start = ((bf16[4,8,4096]{2,1,0:T(8,128)(2,1)}), bf16[4,8,4096]{2,1,0:T(8,128)(2,1)S(1)}, u32[]{:S(2)}, u32[]{:S(2)}) async-start(bf16[4,8,4096]{2,1,0:T(8,128)(2,1)} %block_features.1), calls=%async_computation | async-start | bytes 524288 | tf_op jit(solution)/shard_map/all_to_all | solution.py:171
  19.7 2.9 %collective-permute-start = (bf16[96,4096]{1,0:T(8,128)(2,1)}, bf16[96,4096]{1,0:T(8,128)(2,1)S(1)}, u32[]{:S(2)}, u32[]{:S(2)}) collective-permute-start(bf16[96,4096]{1,0:T(8,128)(2,1)} %param.9), channel_id=1, source_target_pairs={{0,12},{12,0},{1,13},{13,1},{2,14},{14,2},{3,15},{15,3},{4,16},{16... | collective-permute-start | bytes 2359304 | tf_op jit(solution)/shard_map/ppermute | solution.py:17
  22.7 1.3 %fusion.26 = bf16[512,512]{1,0:T(8,128)(2,1)S(1)} fusion(s32[512]{0:T(512)S(1)} %get-tuple-element.18, s32[512]{0:T(512)S(1)} %get-tuple-element.19, s32[512]{0:T(512)S(1)} %get-tuple-element.15, s32[512]{0:T(512)S(1)} %get-tuple-element.20, s32[512]{0:T(512)S(1)} %get-tuple-element.16, s32[512]{0:T(512)S(1)} %get-tuple-element.25, s32[]{:T(128)S(6)} %axis_index.28, ...), kind=kLoop, calls=%fused_computation.61 | loop fusion | flops 21233664 | bytes 542724 | tf_op jit(solution)/shard_map/convert_element_type | solution.py:154
  24.0 6.5 %all-to-all-done = bf16[4,8,4096]{2,1,0:T(8,128)(2,1)S(1)} async-done(((bf16[4,8,4096]{2,1,0:T(8,128)(2,1)}), bf16[4,8,4096]{2,1,0:T(8,128)(2,1)S(1)}, u32[]{:S(2)}, u32[]{:S(2)}) %all-to-all-start) | async-done | bytes 262176 | tf_op jit(solution)/shard_map/all_to_all | solution.py:171
  30.4 5.1 %collective-permute-start.1 = (bf16[32,4096]{1,0:T(8,128)(2,1)S(1)}, bf16[32,4096]{1,0:T(8,128)(2,1)S(1)}, u32[]{:S(2)}, u32[]{:S(2)}) collective-permute-start(bf16[32,4096]{1,0:T(8,128)(2,1)S(1)} %bitcast.27), channel_id=1, source_target_pairs={{0,24},{12,180},{24,48},{36,12},{48,72},{60,36},{72,96},{84,60},{9... | collective-permute-start | bytes 786440 | tf_op jit(solution)/shard_map/ppermute | solution.py:26
  35.5 7.0 %collective-permute-start.2 = (bf16[32,4096]{1,0:T(8,128)(2,1)S(1)}, bf16[32,4096]{1,0:T(8,128)(2,1)S(1)}, u32[]{:S(2)}, u32[]{:S(2)}) collective-permute-start(bf16[32,4096]{1,0:T(8,128)(2,1)S(1)} %bitcast.28), channel_id=1, source_target_pairs={{0,180},{12,24},{24,12},{36,48},{48,36},{60,72},{72,60},{84,96},{9... | collective-permute-start | bytes 786440 | tf_op jit(solution)/shard_map/ppermute | solution.py:26
  42.6 0.3 maximum_select_fusion
  42.9 0.6 fusion.8
  43.5 3.3 %collective-permute-start.3 = (bf16[32,4096]{1,0:T(8,128)(2,1)S(1)}, bf16[32,4096]{1,0:T(8,128)(2,1)S(1)}, u32[]{:S(2)}, u32[]{:S(2)}) collective-permute-start(bf16[32,4096]{1,0:T(8,128)(2,1)S(1)} %collective-permute-done.1), channel_id=1, source_target_pairs={{0,24},{12,180},{24,48},{36,12},{48,72},{60,36},{72,96},{84,60},{9... | collective-permute-start | bytes 786440 | tf_op jit(solution)/shard_map/ppermute | solution.py:26
  46.8 0.6 fusion.7
  47.4 2.5 %collective-permute-start.4 = (bf16[32,4096]{1,0:T(8,128)(2,1)S(1)}, bf16[32,4096]{1,0:T(8,128)(2,1)S(1)}, u32[]{:S(2)}, u32[]{:S(2)}) collective-permute-start(bf16[32,4096]{1,0:T(8,128)(2,1)S(1)} %collective-permute-done.2), channel_id=1, source_target_pairs={{0,24},{12,180},{24,48},{36,12},{48,72},{60,36},{72,96},{84,60},{9... | collective-permute-start | bytes 786440 | tf_op jit(solution)/shard_map/ppermute | solution.py:26
  49.9 0.6 fusion.6
  50.6 4.5 %collective-permute-start.5 = (bf16[32,4096]{1,0:T(8,128)(2,1)S(1)}, bf16[32,4096]{1,0:T(8,128)(2,1)S(1)}, u32[]{:S(2)}, u32[]{:S(2)}) collective-permute-start(bf16[32,4096]{1,0:T(8,128)(2,1)S(1)} %collective-permute-done.3), channel_id=1, source_target_pairs={{0,24},{12,180},{24,48},{36,12},{48,72},{60,36},{72,96},{84,60},{9... | collective-permute-start | bytes 786440 | tf_op jit(solution)/shard_map/ppermute | solution.py:26
  55.1 0.6 fusion.5
  55.7 2.5 %collective-permute-start.6 = (bf16[32,4096]{1,0:T(8,128)(2,1)S(1)}, bf16[32,4096]{1,0:T(8,128)(2,1)S(1)}, u32[]{:S(2)}, u32[]{:S(2)}) collective-permute-start(bf16[32,4096]{1,0:T(8,128)(2,1)S(1)} %collective-permute-done.4), channel_id=1, source_target_pairs={{0,24},{12,180},{24,48},{36,12},{48,72},{60,36},{72,96},{84,60},{9... | collective-permute-start | bytes 786440 | tf_op jit(solution)/shard_map/ppermute | solution.py:26
  58.2 0.6 fusion.4
  58.9 4.5 %collective-permute-start.7 = (bf16[32,4096]{1,0:T(8,128)(2,1)S(1)}, bf16[32,4096]{1,0:T(8,128)(2,1)S(1)}, u32[]{:S(2)}, u32[]{:S(2)}) collective-permute-start(bf16[32,4096]{1,0:T(8,128)(2,1)S(1)} %collective-permute-done.5), channel_id=1, source_target_pairs={{0,24},{12,180},{24,48},{36,12},{48,72},{60,36},{72,96},{84,60},{9... | collective-permute-start | bytes 786440 | tf_op jit(solution)/shard_map/ppermute | solution.py:26
  63.4 0.6 fusion.3
  64.0 0.6 fusion.2
  64.6 2.1 %collective-permute-done.7 = bf16[32,4096]{1,0:T(8,128)(2,1)S(1)} collective-permute-done((bf16[32,4096]{1,0:T(8,128)(2,1)S(1)}, bf16[32,4096]{1,0:T(8,128)(2,1)S(1)}, u32[]{:S(2)}, u32[]{:S(2)}) %collective-permute-start.7) | collective-permute-done | bytes 262176 | tf_op jit(solution)/shard_map/ppermute | solution.py:26
  66.7 0.6 fusion.1
  67.4 20.4 %all_to_all.10 = bf16[24,8,256]{2,1,0:T(8,128)(2,1)S(1)} all-to-all(bf16[24,8,256]{2,1,0:T(8,128)(2,1)S(1)} %bitcast.30), channel_id=1, replica_groups=mesh['zh'=4,'y'=8,'core'=2,'zl'=3,'x'=4] {'core','zl','x'}, dimensions={0} | all-to-all | bytes 196608 | tf_op jit(solution)/shard_map/all_to_all | solution.py:188
  87.9 0.8 fusion
  (17 shorter events, 0.5 us)
Async XLA Ops:
  0.0 42.6 %copy-start = (bf16[96,4096]{1,0:T(8,128)(2,1)S(1)}, bf16[96,4096]{1,0:T(8,128)(2,1)}, u32[]{:S(2)}) copy-start(bf16[96,4096]{1,0:T(8,128)(2,1)} %param.9) | copy-start | bytes 2359300
  4.7 25.8 %all-to-all-start = ((bf16[4,8,4096]{2,1,0:T(8,128)(2,1)}), bf16[4,8,4096]{2,1,0:T(8,128)(2,1)S(1)}, u32[]{:S(2)}, u32[]{:S(2)}) async-start(bf16[4,8,4096]{2,1,0:T(8,128)(2,1)} %block_features.1), calls=%async_computation | async-start | bytes 524288 | tf_op jit(solution)/shard_map/all_to_all | solution.py:171
  19.7 22.8 %collective-permute-start = (bf16[96,4096]{1,0:T(8,128)(2,1)}, bf16[96,4096]{1,0:T(8,128)(2,1)S(1)}, u32[]{:S(2)}, u32[]{:S(2)}) collective-permute-start(bf16[96,4096]{1,0:T(8,128)(2,1)} %param.9), channel_id=1, source_target_pairs={{0,12},{12,0},{1,13},{13,1},{2,14},{14,2},{3,15},{15,3},{4,16},{16... | collective-permute-start | bytes 2359304 | tf_op jit(solution)/shard_map/ppermute | solution.py:17
  30.4 13.1 %collective-permute-start.1 = (bf16[32,4096]{1,0:T(8,128)(2,1)S(1)}, bf16[32,4096]{1,0:T(8,128)(2,1)S(1)}, u32[]{:S(2)}, u32[]{:S(2)}) collective-permute-start(bf16[32,4096]{1,0:T(8,128)(2,1)S(1)} %bitcast.27), channel_id=1, source_target_pairs={{0,24},{12,180},{24,48},{36,12},{48,72},{60,36},{72,96},{84,60},{9... | collective-permute-start | bytes 786440 | tf_op jit(solution)/shard_map/ppermute | solution.py:26
  35.5 11.9 %collective-permute-start.2 = (bf16[32,4096]{1,0:T(8,128)(2,1)S(1)}, bf16[32,4096]{1,0:T(8,128)(2,1)S(1)}, u32[]{:S(2)}, u32[]{:S(2)}) collective-permute-start(bf16[32,4096]{1,0:T(8,128)(2,1)S(1)} %bitcast.28), channel_id=1, source_target_pairs={{0,180},{12,24},{24,12},{36,48},{48,36},{60,72},{72,60},{84,96},{9... | collective-permute-start | bytes 786440 | tf_op jit(solution)/shard_map/ppermute | solution.py:26
  43.5 7.1 %collective-permute-start.3 = (bf16[32,4096]{1,0:T(8,128)(2,1)S(1)}, bf16[32,4096]{1,0:T(8,128)(2,1)S(1)}, u32[]{:S(2)}, u32[]{:S(2)}) collective-permute-start(bf16[32,4096]{1,0:T(8,128)(2,1)S(1)} %collective-permute-done.1), channel_id=1, source_target_pairs={{0,24},{12,180},{24,48},{36,12},{48,72},{60,36},{72,96},{84,60},{9... | collective-permute-start | bytes 786440 | tf_op jit(solution)/shard_map/ppermute | solution.py:26
  47.4 8.3 %collective-permute-start.4 = (bf16[32,4096]{1,0:T(8,128)(2,1)S(1)}, bf16[32,4096]{1,0:T(8,128)(2,1)S(1)}, u32[]{:S(2)}, u32[]{:S(2)}) collective-permute-start(bf16[32,4096]{1,0:T(8,128)(2,1)S(1)} %collective-permute-done.2), channel_id=1, source_target_pairs={{0,24},{12,180},{24,48},{36,12},{48,72},{60,36},{72,96},{84,60},{9... | collective-permute-start | bytes 786440 | tf_op jit(solution)/shard_map/ppermute | solution.py:26
  50.6 8.3 %collective-permute-start.5 = (bf16[32,4096]{1,0:T(8,128)(2,1)S(1)}, bf16[32,4096]{1,0:T(8,128)(2,1)S(1)}, u32[]{:S(2)}, u32[]{:S(2)}) collective-permute-start(bf16[32,4096]{1,0:T(8,128)(2,1)S(1)} %collective-permute-done.3), channel_id=1, source_target_pairs={{0,24},{12,180},{24,48},{36,12},{48,72},{60,36},{72,96},{84,60},{9... | collective-permute-start | bytes 786440 | tf_op jit(solution)/shard_map/ppermute | solution.py:26
  55.7 8.3 %collective-permute-start.6 = (bf16[32,4096]{1,0:T(8,128)(2,1)S(1)}, bf16[32,4096]{1,0:T(8,128)(2,1)S(1)}, u32[]{:S(2)}, u32[]{:S(2)}) collective-permute-start(bf16[32,4096]{1,0:T(8,128)(2,1)S(1)} %collective-permute-done.4), channel_id=1, source_target_pairs={{0,24},{12,180},{24,48},{36,12},{48,72},{60,36},{72,96},{84,60},{9... | collective-permute-start | bytes 786440 | tf_op jit(solution)/shard_map/ppermute | solution.py:26
  58.9 7.8 %collective-permute-start.7 = (bf16[32,4096]{1,0:T(8,128)(2,1)S(1)}, bf16[32,4096]{1,0:T(8,128)(2,1)S(1)}, u32[]{:S(2)}, u32[]{:S(2)}) collective-permute-start(bf16[32,4096]{1,0:T(8,128)(2,1)S(1)} %collective-permute-done.5), channel_id=1, source_target_pairs={{0,24},{12,180},{24,48},{36,12},{48,72},{60,36},{72,96},{84,60},{9... | collective-permute-start | bytes 786440 | tf_op jit(solution)/shard_map/ppermute | solution.py:26

commit v8 on v6

--- a/solution.py
+++ b/solution.py
@@ -111,7 +111,7 @@
     core = source // (EX_DEV * Z_HI * Y)
     away = (piece + 1) // 2
     from_y = (y + jnp.where(core == 0, Y - away, away)) % Y
-    from_core = jnp.where((piece % 2 == 1) | (piece == 0), core, 1 - core)
+    from_core = jnp.where(piece % 2 == 0, core, 1 - core)
     return (result == ((z_hi * Y + from_y) * CORE + from_core) * EX_DEV + example).astype(
         jnp.bfloat16
     )
@@ -135,26 +135,23 @@
     place = placing(CORE * Y * Z_HI * EX_DEV, y)
     mine, place = lax.optimization_barrier((mine, place))
 
-    near, cross = onward(mine), onward(mine, swap=True)
-    pieces = [mine, near, cross]
+    cross, near = onward(mine, swap=True), onward(mine)
+    pieces = [mine, cross, near]
     for _ in (2, 3):
-        near, cross = onward(near), onward(cross)
-        pieces += [near, cross]
-    pieces.append(onward(near))
+        cross, near = onward(cross), onward(near)
+        pieces += [cross, near]
+    pieces.append(onward(cross))
 
     scores = [scored(queries, piece) for piece in pieces]
     members = Z_LO * X
     parts = jnp.concatenate([part.astype(jnp.bfloat16) for part in scores], axis=1)
     parts = parts.reshape(CORE * members, rows // members, -1)
     traded = lax.all_to_all(parts, ("core",) + MP, 0, 0, tiled=False).reshape(CORE, rows, -1)
-    placed = sum(
-        lax.dot_general(
-            traded[i],
-            place[i * traded.shape[2] : (i + 1) * traded.shape[2]],
-            (((1,), (0,)), ((), ())),
-            preferred_element_type=jnp.float32,
-        )
-        for i in range(CORE)
+    placed = lax.dot_general(
+        jnp.concatenate([traded[i] for i in range(CORE)], axis=1),
+        place,
+        (((1,), (0,)), ((), ())),
+        preferred_element_type=jnp.float32,
     )
     return jnp.sum(placed.reshape(members, rows // members, -1), axis=0)
 

time: 88.2 us -> 87.1 us (0.988)
  blocking collectives: 20.5 us -> 19 us
    all_to_all x1, blocking collectives: 20.5 us -> 19 us  [shards(): lax.all_to_all(parts, ('core',) + MP, 0, 0, tiled=False)]
  transfers between devices with their start and end apart: 9 -> 9, of which waited for: 4 -> 3; matrix products, arithmetic and copies ran while one was open for 7% -> 7% of each run, Pallas kernels for 0% -> 0%
where the time goes in v8:
time: 87.1 us; the launch traced here: 86.6 us
  starting transfers between devices  47.8 us (55%)
  blocking collectives  19 us (22%)
  waiting for transfers between devices  8.84 us (10%)
  matrix products  5.47 us (6%)
  Pallas kernels  3.6 us (4%)
  other arithmetic  1.66 us (2%)
    ppermute x7, starting transfers between devices, onward(): return lax.ppermute(array, ('y', 'core'), pairs)  29.9 us
    all_to_all x1, blocking collectives, shards(): lax.all_to_all(parts, ('core',) + MP, 0, 0, tiled=False)  19 us
    all_to_all x1, starting transfers between devices, shards(): lax.all_to_all(features, 'zh', 0, 0, tiled=False)  15 us
    all_to_all x1, waiting for transfers between devices, shards(): lax.all_to_all(features, 'zh', 0, 0, tiled=False)  6.45 us
    dot_general x8, matrix products, scored(): lax.dot_general(queries, pieces, (((1,), (1,)), ((), ())), preferred_elem...  4.65 us
    pallas_call x1, Pallas kernels, block_features(): pl.pallas_call(features_kernel, out_shape=jax.ShapeDtypeStruct((Z_HI, EX_...  3.6 us
    ppermute x1, starting transfers between devices, from_behind(): lax.ppermute(array, axis, [(i, (i + by) % length) for i in range(length)])  2.85 us
    ppermute x7, waiting for transfers between devices, onward(): return lax.ppermute(array, ('y', 'core'), pairs)  2.38 us
  transfers between devices with their start and end apart: 9, of which 3 were waited for; matrix products, arithmetic and copies ran while one was open for 7% of the time, Pallas kernels for 0%

profile of v8, /device:TPU:1, one launch (start us, length us, event | category | flops | bytes accessed | tf_op | source)
XLA Modules:
  0.0 86.6 jit_solution(16464490085350544495)
XLA Ops:
  0.0 3.6 %block_features.1 = bf16[4,8,4096]{2,1,0:T(8,128)(2,1)} custom-call(bf16[1,2048,128]{2,1,0:T(8,128)(2,1)} %token_ref.1, s32[1,2048]{1,0:T(1,128)} %label_ref.1, bf16[1,64,64]{2,1,0:T(8,128)(2,1)} %left_ref.1, bf16[1,64,64]{2,1,0:T(8,128)(2,1)} %right_ref.1), custom_call_target="tpu_custom_call" | custom-call | flops 268435456 | bytes 786432 | tf_op jit(solution)/shard_map/block_features/pallas_call | solution.py:84
  3.6 15.0 %all-to-all-start = ((bf16[4,8,4096]{2,1,0:T(8,128)(2,1)}), bf16[4,8,4096]{2,1,0:T(8,128)(2,1)S(1)}, u32[]{:S(2)}, u32[]{:S(2)}) async-start(bf16[4,8,4096]{2,1,0:T(8,128)(2,1)} %block_features.1), calls=%async_computation | async-start | bytes 524288 | tf_op jit(solution)/shard_map/all_to_all | solution.py:132
  18.6 2.9 %collective-permute-start = (bf16[96,4096]{1,0:T(8,128)(2,1)}, bf16[96,4096]{1,0:T(8,128)(2,1)S(1)}, u32[]{:S(2)}, u32[]{:S(2)}) collective-permute-start(bf16[96,4096]{1,0:T(8,128)(2,1)} %param.9), channel_id=1, source_target_pairs={{0,12},{12,0},{1,13},{13,1},{2,14},{14,2},{3,15},{15,3},{4,16},{16... | collective-permute-start | bytes 2359304 | tf_op jit(solution)/shard_map/ppermute | solution.py:16
  21.6 1.3 %fusion.24 = bf16[512,512]{1,0:T(8,128)(2,1)S(1)} fusion(s32[512]{0:T(512)S(1)} %get-tuple-element.18, s32[512]{0:T(512)S(1)} %get-tuple-element.19, s32[512]{0:T(512)S(1)} %get-tuple-element.15, s32[512]{0:T(512)S(1)} %get-tuple-element.20, s32[512]{0:T(512)S(1)} %get-tuple-element.16, s32[512]{0:T(512)S(1)} %get-tuple-element.25, s32[]{:T(128)S(6)} %axis_index.28, ...), kind=kLoop, calls=%fused_computation.59 | loop fusion | flops 20709376 | bytes 542724 | tf_op jit(solution)/shard_map/convert_element_type | solution.py:115
  22.9 6.5 %all-to-all-done = bf16[4,8,4096]{2,1,0:T(8,128)(2,1)S(1)} async-done(((bf16[4,8,4096]{2,1,0:T(8,128)(2,1)}), bf16[4,8,4096]{2,1,0:T(8,128)(2,1)S(1)}, u32[]{:S(2)}, u32[]{:S(2)}) %all-to-all-start) | async-done | bytes 262176 | tf_op jit(solution)/shard_map/all_to_all | solution.py:132
  29.4 8.6 %collective-permute-start.1 = (bf16[32,4096]{1,0:T(8,128)(2,1)S(1)}, bf16[32,4096]{1,0:T(8,128)(2,1)S(1)}, u32[]{:S(2)}, u32[]{:S(2)}) collective-permute-start(bf16[32,4096]{1,0:T(8,128)(2,1)S(1)} %bitcast.27), channel_id=1, source_target_pairs={{0,180},{12,24},{24,12},{36,48},{48,36},{60,72},{72,60},{84,96},{9... | collective-permute-start | bytes 786440 | tf_op jit(solution)/shard_map/ppermute | solution.py:25
  38.0 3.3 %collective-permute-start.2 = (bf16[32,4096]{1,0:T(8,128)(2,1)S(1)}, bf16[32,4096]{1,0:T(8,128)(2,1)S(1)}, u32[]{:S(2)}, u32[]{:S(2)}) collective-permute-start(bf16[32,4096]{1,0:T(8,128)(2,1)S(1)} %bitcast.28), channel_id=1, source_target_pairs={{0,24},{12,180},{24,48},{36,12},{48,72},{60,36},{72,96},{84,60},{9... | collective-permute-start | bytes 786440 | tf_op jit(solution)/shard_map/ppermute | solution.py:25
  41.3 0.3 maximum_select_fusion
  41.6 0.6 fusion.8
  42.3 3.8 %collective-permute-start.3 = (bf16[32,4096]{1,0:T(8,128)(2,1)S(1)}, bf16[32,4096]{1,0:T(8,128)(2,1)S(1)}, u32[]{:S(2)}, u32[]{:S(2)}) collective-permute-start(bf16[32,4096]{1,0:T(8,128)(2,1)S(1)} %collective-permute-done.1), channel_id=1, source_target_pairs={{0,24},{12,180},{24,48},{36,12},{48,72},{60,36},{72,96},{84,60},{9... | collective-permute-start | bytes 786440 | tf_op jit(solution)/shard_map/ppermute | solution.py:25
  46.1 0.6 fusion.7
  46.7 3.4 %collective-permute-start.4 = (bf16[32,4096]{1,0:T(8,128)(2,1)S(1)}, bf16[32,4096]{1,0:T(8,128)(2,1)S(1)}, u32[]{:S(2)}, u32[]{:S(2)}) collective-permute-start(bf16[32,4096]{1,0:T(8,128)(2,1)S(1)} %collective-permute-done.2), channel_id=1, source_target_pairs={{0,24},{12,180},{24,48},{36,12},{48,72},{60,36},{72,96},{84,60},{9... | collective-permute-start | bytes 786440 | tf_op jit(solution)/shard_map/ppermute | solution.py:25
  50.1 0.6 fusion.6
  50.7 3.7 %collective-permute-start.5 = (bf16[32,4096]{1,0:T(8,128)(2,1)S(1)}, bf16[32,4096]{1,0:T(8,128)(2,1)S(1)}, u32[]{:S(2)}, u32[]{:S(2)}) collective-permute-start(bf16[32,4096]{1,0:T(8,128)(2,1)S(1)} %collective-permute-done.3), channel_id=1, source_target_pairs={{0,24},{12,180},{24,48},{36,12},{48,72},{60,36},{72,96},{84,60},{9... | collective-permute-start | bytes 786440 | tf_op jit(solution)/shard_map/ppermute | solution.py:25
  54.4 0.6 fusion.5
  55.0 3.4 %collective-permute-start.6 = (bf16[32,4096]{1,0:T(8,128)(2,1)S(1)}, bf16[32,4096]{1,0:T(8,128)(2,1)S(1)}, u32[]{:S(2)}, u32[]{:S(2)}) collective-permute-start(bf16[32,4096]{1,0:T(8,128)(2,1)S(1)} %collective-permute-done.4), channel_id=1, source_target_pairs={{0,24},{12,180},{24,48},{36,12},{48,72},{60,36},{72,96},{84,60},{9... | collective-permute-start | bytes 786440 | tf_op jit(solution)/shard_map/ppermute | solution.py:25
  58.4 0.6 fusion.4
  59.0 3.7 %collective-permute-start.7 = (bf16[32,4096]{1,0:T(8,128)(2,1)S(1)}, bf16[32,4096]{1,0:T(8,128)(2,1)S(1)}, u32[]{:S(2)}, u32[]{:S(2)}) collective-permute-start(bf16[32,4096]{1,0:T(8,128)(2,1)S(1)} %collective-permute-done.5), channel_id=1, source_target_pairs={{0,24},{12,180},{24,48},{36,12},{48,72},{60,36},{72,96},{84,60},{9... | collective-permute-start | bytes 786440 | tf_op jit(solution)/shard_map/ppermute | solution.py:25
  62.8 0.6 fusion.3
  63.4 0.6 fusion.2
  63.9 2.2 %collective-permute-done.7 = bf16[32,4096]{1,0:T(8,128)(2,1)S(1)} collective-permute-done((bf16[32,4096]{1,0:T(8,128)(2,1)S(1)}, bf16[32,4096]{1,0:T(8,128)(2,1)S(1)}, u32[]{:S(2)}, u32[]{:S(2)}) %collective-permute-start.7) | collective-permute-done | bytes 262176 | tf_op jit(solution)/shard_map/ppermute | solution.py:25
  66.1 0.6 fusion.1
  66.8 19.0 %all_to_all.10 = bf16[24,8,256]{2,1,0:T(8,128)(2,1)S(1)} all-to-all(bf16[24,8,256]{2,1,0:T(8,128)(2,1)S(1)} %bitcast.30), channel_id=1, replica_groups=mesh['zh'=4,'y'=8,'core'=2,'zl'=3,'x'=4] {'core','zl','x'}, dimensions={0} | all-to-all | bytes 196608 | tf_op jit(solution)/shard_map/all_to_all | solution.py:149
  85.8 0.8 fusion
  (17 shorter events, 0.3 us)
Async XLA Ops:
  0.0 41.3 %copy-start = (bf16[96,4096]{1,0:T(8,128)(2,1)S(1)}, bf16[96,4096]{1,0:T(8,128)(2,1)}, u32[]{:S(2)}) copy-start(bf16[96,4096]{1,0:T(8,128)(2,1)} %param.9) | copy-start | bytes 2359300
  3.6 25.8 %all-to-all-start = ((bf16[4,8,4096]{2,1,0:T(8,128)(2,1)}), bf16[4,8,4096]{2,1,0:T(8,128)(2,1)S(1)}, u32[]{:S(2)}, u32[]{:S(2)}) async-start(bf16[4,8,4096]{2,1,0:T(8,128)(2,1)} %block_features.1), calls=%async_computation | async-start | bytes 524288 | tf_op jit(solution)/shard_map/all_to_all | solution.py:132
  18.6 22.6 %collective-permute-start = (bf16[96,4096]{1,0:T(8,128)(2,1)}, bf16[96,4096]{1,0:T(8,128)(2,1)S(1)}, u32[]{:S(2)}, u32[]{:S(2)}) collective-permute-start(bf16[96,4096]{1,0:T(8,128)(2,1)} %param.9), channel_id=1, source_target_pairs={{0,12},{12,0},{1,13},{13,1},{2,14},{14,2},{3,15},{15,3},{4,16},{16... | collective-permute-start | bytes 2359304 | tf_op jit(solution)/shard_map/ppermute | solution.py:16
  29.4 12.9 %collective-permute-start.1 = (bf16[32,4096]{1,0:T(8,128)(2,1)S(1)}, bf16[32,4096]{1,0:T(8,128)(2,1)S(1)}, u32[]{:S(2)}, u32[]{:S(2)}) collective-permute-start(bf16[32,4096]{1,0:T(8,128)(2,1)S(1)} %bitcast.27), channel_id=1, source_target_pairs={{0,180},{12,24},{24,12},{36,48},{48,36},{60,72},{72,60},{84,96},{9... | collective-permute-start | bytes 786440 | tf_op jit(solution)/shard_map/ppermute | solution.py:25
  38.0 8.7 %collective-permute-start.2 = (bf16[32,4096]{1,0:T(8,128)(2,1)S(1)}, bf16[32,4096]{1,0:T(8,128)(2,1)S(1)}, u32[]{:S(2)}, u32[]{:S(2)}) collective-permute-start(bf16[32,4096]{1,0:T(8,128)(2,1)S(1)} %bitcast.28), channel_id=1, source_target_pairs={{0,24},{12,180},{24,48},{36,12},{48,72},{60,36},{72,96},{84,60},{9... | collective-permute-start | bytes 786440 | tf_op jit(solution)/shard_map/ppermute | solution.py:25
  42.3 8.4 %collective-permute-start.3 = (bf16[32,4096]{1,0:T(8,128)(2,1)S(1)}, bf16[32,4096]{1,0:T(8,128)(2,1)S(1)}, u32[]{:S(2)}, u32[]{:S(2)}) collective-permute-start(bf16[32,4096]{1,0:T(8,128)(2,1)S(1)} %collective-permute-done.1), channel_id=1, source_target_pairs={{0,24},{12,180},{24,48},{36,12},{48,72},{60,36},{72,96},{84,60},{9... | collective-permute-start | bytes 786440 | tf_op jit(solution)/shard_map/ppermute | solution.py:25
  46.7 8.3 %collective-permute-start.4 = (bf16[32,4096]{1,0:T(8,128)(2,1)S(1)}, bf16[32,4096]{1,0:T(8,128)(2,1)S(1)}, u32[]{:S(2)}, u32[]{:S(2)}) collective-permute-start(bf16[32,4096]{1,0:T(8,128)(2,1)S(1)} %collective-permute-done.2), channel_id=1, source_target_pairs={{0,24},{12,180},{24,48},{36,12},{48,72},{60,36},{72,96},{84,60},{9... | collective-permute-start | bytes 786440 | tf_op jit(solution)/shard_map/ppermute | solution.py:25
  50.7 8.3 %collective-permute-start.5 = (bf16[32,4096]{1,0:T(8,128)(2,1)S(1)}, bf16[32,4096]{1,0:T(8,128)(2,1)S(1)}, u32[]{:S(2)}, u32[]{:S(2)}) collective-permute-start(bf16[32,4096]{1,0:T(8,128)(2,1)S(1)} %collective-permute-done.3), channel_id=1, source_target_pairs={{0,24},{12,180},{24,48},{36,12},{48,72},{60,36},{72,96},{84,60},{9... | collective-permute-start | bytes 786440 | tf_op jit(solution)/shard_map/ppermute | solution.py:25
  55.0 8.3 %collective-permute-start.6 = (bf16[32,4096]{1,0:T(8,128)(2,1)S(1)}, bf16[32,4096]{1,0:T(8,128)(2,1)S(1)}, u32[]{:S(2)}, u32[]{:S(2)}) collective-permute-start(bf16[32,4096]{1,0:T(8,128)(2,1)S(1)} %collective-permute-done.4), channel_id=1, source_target_pairs={{0,24},{12,180},{24,48},{36,12},{48,72},{60,36},{72,96},{84,60},{9... | collective-permute-start | bytes 786440 | tf_op jit(solution)/shard_map/ppermute | solution.py:25
  59.0 7.1 %collective-permute-start.7 = (bf16[32,4096]{1,0:T(8,128)(2,1)S(1)}, bf16[32,4096]{1,0:T(8,128)(2,1)S(1)}, u32[]{:S(2)}, u32[]{:S(2)}) collective-permute-start(bf16[32,4096]{1,0:T(8,128)(2,1)S(1)} %collective-permute-done.5), channel_id=1, source_target_pairs={{0,24},{12,180},{24,48},{36,12},{48,72},{60,36},{72,96},{84,60},{9... | collective-permute-start | bytes 786440 | tf_op jit(solution)/shard_map/ppermute | solution.py:25
